TPU v7x, 32 devices: a whole 2x2x4 slice. The times are simulated.
32 devices in a mesh: depth: 4 (over y, core), image: 8 (over z, x).
Axes of the slice: x: 2, y: 2, z: 4, core: 2. Of those that a mesh axis runs over, the one named last changes fastest.
Arguments:
- populations: float32 [19, 128, 128, 128], P(None, 'depth', 'image'), may hold values from 0 to 0.4, as said below
- transfer: float32 [8, 5, 8], P('image'), may hold values from 0.1 to 1
- direction: int32 [8], P('image'), may hold values from 0 to 1
Outputs:
- final_populations: float32 [19, 128, 128, 128], P(None, 'depth', 'image')
- vorticity: bfloat16 [128, 128, 128], P('depth', 'image')
- images: float32 [8, 4, 128, 128], P('image', None, 'depth')
Inputs may be any that keep to these rules, and one draw needn't show every extreme that they name: `populations`: each population is positive, its lattice weight times a density near one with a perturbation by a rough flow of small speed. `direction`: 0 views from the side of small x, 1 from the side of large x.
All inputs are finite; a program needn't handle non-finite values.
Results may differ from a plain program's by a relative error of at most 0.001.
Values may be sent and summed in bfloat16 or wider, within the bound.
A program may use at most 128 MiB of HBM per device.

v0:
```python
import jax
import jax.numpy as jnp
import numpy as np
from jax import lax
from jax.sharding import PartitionSpec as P

STEPS = 4


lattice_velocities = (
    (0, 0, 0),
    (1, 0, 0),
    (-1, 0, 0),
    (0, 1, 0),
    (0, -1, 0),
    (0, 0, 1),
    (0, 0, -1),
    (1, 1, 0),
    (-1, -1, 0),
    (1, -1, 0),
    (-1, 1, 0),
    (1, 0, 1),
    (-1, 0, -1),
    (1, 0, -1),
    (-1, 0, 1),
    (0, 1, 1),
    (0, -1, -1),
    (0, 1, -1),
    (0, -1, 1),
)
lattice_weights = (1.0 / 3.0,) + (1.0 / 18.0,) * 6 + (1.0 / 36.0,) * 12
relaxation = 1.25
bump_width = 0.15
level_offset = 0.05


def with_halo(shard, sides, width):
    for axis, dim in sides:
        devices, length = (lax.axis_size(axis), shard.shape[dim])
        up = [(i, (i + 1) % devices) for i in range(devices)]
        down = [(j, i) for i, j in up]
        last = lax.slice_in_dim(shard, length - width, length, axis=dim)
        first = lax.slice_in_dim(shard, 0, width, axis=dim)
        before = lax.ppermute(last, axis, up)
        after = lax.ppermute(first, axis, down)
        shard = jnp.concatenate([before, shard, after], axis=dim)
    return shard


def from_partner(block, axis, distance):
    count = lax.axis_size(axis)
    route = []
    for low in range(count):
        high = low | 1 << distance
        if high != low and high < count:
            route += [(low, high), (high, low)]
    return lax.ppermute(block, axis, route)


def moments(field):
    density = field[0]
    for number in range(1, 19):
        density = density + field[number]
    components = []
    for axis_index in range(3):
        total = jnp.zeros_like(density)
        for number in range(19):
            factor = lattice_velocities[number][axis_index]
            if factor != 0:
                total = total + factor * field[number]
        components.append(total / density)
    return (density, components)


def collide(field):
    density, flow = moments(field)
    squared = flow[0] * flow[0] + flow[1] * flow[1] + flow[2] * flow[2]
    result = []
    for number in range(19):
        project = jnp.zeros_like(density)
        for axis_index in range(3):
            factor = lattice_velocities[number][axis_index]
            if factor != 0:
                project = project + factor * flow[axis_index]
        equilibrium = (
            lattice_weights[number]
            * density
            * (1.0 + 3.0 * project + 4.5 * project * project - 1.5 * squared)
        )
        result.append(field[number] - relaxation * (field[number] - equilibrium))
    return jnp.stack(result)


def stream(padded, depth_cells, width_cells):
    pieces = []
    for number in range(19):
        shift_x, shift_y, shift_z = lattice_velocities[number]
        window = padded[
            number,
            1 - shift_x : 1 - shift_x + depth_cells,
            1 - shift_y : 1 - shift_y + width_cells,
            :,
        ]
        if shift_z != 0:
            window = jnp.roll(window, shift_z, axis=2)
        pieces.append(window)
    return jnp.stack(pieces)


def spin_magnitude(field):
    density, flow = moments(field)
    padded = with_halo(jnp.stack(flow), (("depth", 1), ("image", 2)), 1)
    inner = padded[:, 1:-1, 1:-1, :]

    def across_x(component):
        return (padded[component, 2:, 1:-1, :] - padded[component, :-2, 1:-1, :]) * 0.5

    def across_y(component):
        return (padded[component, 1:-1, 2:, :] - padded[component, 1:-1, :-2, :]) * 0.5

    def across_z(component):
        return (jnp.roll(inner[component], -1, 2) - jnp.roll(inner[component], 1, 2)) * 0.5

    spin_x = across_y(2) - across_z(1)
    spin_y = across_z(0) - across_x(2)
    spin_z = across_x(1) - across_y(0)
    return jnp.sqrt(spin_x * spin_x + spin_y * spin_y + spin_z * spin_z).astype(jnp.bfloat16)


def render_block(level, params, backward, ray_cells):
    extinction = jnp.zeros_like(level)
    emission = [jnp.zeros_like(level) for channel in range(3)]
    for bump_index in range(params.shape[1]):
        bump = jnp.exp(-jnp.square((level - params[0, bump_index]) / bump_width))
        extinction = extinction + params[1, bump_index] * bump
        for channel in range(3):
            emission[channel] = emission[channel] + params[2 + channel, bump_index] * bump
    optical = extinction / ray_cells
    inclusive = jnp.cumsum(optical, axis=0)
    total = inclusive[-1]
    front = jnp.where(backward, total[None] - inclusive, inclusive - optical)
    weight = jnp.exp(-front) * (1.0 - jnp.exp(-optical))
    colors = [jnp.sum(weight * emission[channel], axis=0) for channel in range(3)]
    return jnp.stack(colors + [jnp.exp(-total)])


def render_many(brick, params, backward, ray_cells):
    level = brick.astype(jnp.float32)
    level = level / (level + level_offset)

    def render_single(pair):
        return render_block(level, pair[0], pair[1], ray_cells)

    return lax.map(render_single, (params, backward))


def over(front_part, back_part):
    colors = front_part[:, :3] + front_part[:, 3:4] * back_part[:, :3]
    return jnp.concatenate([colors, front_part[:, 3:4] * back_part[:, 3:4]], axis=1)


def reversed_order(count, levels):
    order = []
    for number in range(count):
        value = 0
        for section_bit in range(levels):
            if number >> section_bit & 1:
                value = value | 1 << levels - 1 - section_bit
        order.append(value)
    return np.array(order, dtype=np.int32)


def composite_pairs(fragments, backward):
    slab_total = lax.axis_size("depth")
    levels = slab_total.bit_length() - 1
    tf_count, channels, rows, cells = fragments.shape
    blocks = fragments.reshape(tf_count, channels, slab_total, rows // slab_total, cells)
    current = blocks[:, :, reversed_order(slab_total, levels)].reshape(fragments.shape)
    position = lax.axis_index("depth")
    chooser = backward[:, None, None, None]
    for section_bit in range(levels):
        half = current.shape[2] // 2
        lower = current[:, :, :half]
        upper = current[:, :, half:]
        bit_set = jnp.bitwise_and(jnp.right_shift(position, section_bit), 1) == 1
        kept = jnp.where(bit_set, upper, lower)
        sent = jnp.where(bit_set, lower, upper)
        received = from_partner(sent, "depth", section_bit)
        mine_front = chooser == bit_set
        current = jnp.where(mine_front, over(kept, received), over(received, kept))
    return current


def on_device(populations, transfer, direction):
    depth_cells = populations.shape[1]
    width_cells = populations.shape[2]
    field = populations
    for turn_index in range(STEPS):
        collided = collide(field)
        padded = with_halo(collided, (("depth", 1), ("image", 2)), 1)
        field = stream(padded, depth_cells, width_cells)
    vorticity = spin_magnitude(field)
    ray_cells = depth_cells * lax.axis_size("depth")
    backward = direction == 1
    fragments = render_many(
        lax.all_gather(vorticity, "image", axis=1, tiled=True), transfer, backward, ray_cells
    )
    combined = composite_pairs(fragments, backward)
    images = jnp.concatenate([combined[:, :3], 1.0 - combined[:, 3:4]], axis=1)
    return (field, vorticity, images)


def solution(mesh):
    in_specs = (P(None, "depth", "image", None), P("image", None, None), P("image"))
    out_specs = (
        P(None, "depth", "image", None),
        P("depth", "image", None),
        P("image", None, "depth", None),
    )
    return jax.shard_map(
        on_device, mesh=mesh, in_specs=in_specs, out_specs=out_specs, check_vma=False
    )
```

profile of v0, /device:TPU:0, one launch (start us, length us, event | category | flops | bytes accessed | tf_op | source)
XLA Modules:
  0.0 373.2 jit_solution(14949431008369657655)
XLA Ops:
  7.2 3.9 %constant_dynamic-update-slice_fusion = (f32[19,32,16,128]{3,2,1,0:T(8,128)S(1)}, f32[1,32,16,128]{3,2,1,0:T(8,128)}, f32[1,32,16,128]{3,2,1,0:T(8,128)S(1)}, f3...) fusion(f32[19,32,16,128]{3,2,1,0:T(8,128)} %param.5), kind=kLoop, calls=%fused_computation.1070 | loop fusion | flops 4718591 | bytes 6815744
  13.9 2.0 collective-permute-start.1
  19.0 1.0 slice_bitcast_fusion.43
  20.2 3.9 %pad_maximum_fusion.11 = (f32[19,34,1,128]{3,2,1,0:T(1,128)}, f32[19,34,1,128]{3,2,1,0:T(1,128)}) fusion(f32[19,1,16,128]{3,2,1,0:T(8,128)S(1)} %collective-permute-done.1, f32[19,32,16,128]{3,2,1,0:T(8,128)} %copy-done.4, f32[19,1,16,128]{3,2,1,0:T(8,128)S(1)} %collective-permute-done), kind=kLoop, calls=%fused_computation.90 | loop fusion | flops 330752 | bytes 5953536 | tf_op jit(solution)/shard_map/slice | solution.py:42
  24.2 2.1 collective-permute-start.2
  26.3 3.3 collective-permute-start.3
  29.6 1.1 slice_bitcast_fusion.41
  35.3 1.0 slice_bitcast_fusion.39
  36.4 4.9 %collective-permute-done.2 = f32[19,34,1,128]{3,2,1,0:T(1,128)S(1)} collective-permute-done((f32[19,34,1,128]{3,2,1,0:T(1,128)}, f32[19,34,1,128]{3,2,1,0:T(1,128)S(1)}, u32[]{:S(2)}, u32[]{:S(2)}) %collective-permute-start.2) | collective-permute-done | bytes 330784 | tf_op jit(solution)/shard_map/ppermute | solution.py:44
  41.3 2.2 collective-permute-done.3
  43.5 1.5 maximum_bitcast_fusion.13
  45.2 1.1 slice_bitcast_fusion.37
  46.4 1.1 slice_bitcast_fusion.35
  48.2 5.3 %fusion.221 = (f32[32,16,128]{2,1,0:T(8,128)}, f32[32,16,128]{2,1,0:T(8,128)S(1)}, f32[32,16,128]{2,1,0:T(8,128)S(1)}, f32[32,16,128]{2,1,0:T(8,128)S(1)}, f32[3...) fusion(f32[32,16,127]{2,1,0:T(8,128)} %get-tuple-element.343, ...), kind=kLoop, calls=%fused_computation.312 | loop fusion | flops 7405568 | bytes 12769280 | tf_op jit(solution)/shard_map/sub | solution.py:90
  57.6 4.2 %constant_dynamic-update-slice_fusion.1 = (f32[19,32,16,128]{3,2,1,0:T(8,128)S(1)}, f32[1,32,16,128]{3,2,1,0:T(8,128)}, f32[1,32,16,128]{3,2,1,0:T(8,128)S(1)}, ...) fusion(f32[1,32,16,128]{3,2,1,0:T(8,128)} %get-tuple-element.11, ...), kind=kLoop, calls=%fused_computation.1071 | loop fusion | flops 5373951 | bytes 8912896
  65.0 2.3 copy-done.3
  67.3 1.7 collective-permute-start.5
  72.6 1.6 maximum_bitcast_fusion.11
  76.0 1.3 pad_maximum_fusion.8
  77.6 4.7 %collective-permute-start.7 = (f32[19,34,1,128]{3,2,1,0:T(1,128)}, f32[19,34,1,128]{3,2,1,0:T(1,128)}, u32[]{:S(2)}, u32[]{:S(2)}) collective-permute-start(f32[19,34,1,128]{3,2,1,0:T(1,128)} %get-tuple-element.150), channel_id=1, source_target_pairs={{1,0},{2,1},{3,2},{4,3},{5,4},{6,5},{7,6},{0,7},{9,8},{10,9},{11,1... | collective-permute-start | bytes 992264 | tf_op jit(solution)/shard_map/ppermute | solution.py:45
  88.7 4.3 %collective-permute-done.6 = f32[19,34,1,128]{3,2,1,0:T(1,128)} collective-permute-done((f32[19,34,1,128]{3,2,1,0:T(1,128)}, f32[19,34,1,128]{3,2,1,0:T(1,128)}, u32[]{:S(2)}, u32[]{:S(2)}) %collective-permute-start.6) | collective-permute-done | bytes 330784 | tf_op jit(solution)/shard_map/ppermute | solution.py:44
  93.0 2.9 collective-permute-done.7
  95.9 1.4 maximum_bitcast_fusion.9
  105.7 4.2 %fusion.332 = (f32[32,16,128]{2,1,0:T(8,128)S(1)}, f32[32,16,128]{2,1,0:T(8,128)S(1)}, f32[32,16,128]{2,1,0:T(8,128)S(1)}, f32[32,16,128]{2,1,0:T(8,128)S(1)}, f...) fusion(f32[32,16,127]{2,1,0:T(8,128)} %get-tuple-element.262, ...), kind=kLoop, calls=%fused_computation.423 | loop fusion | flops 7405568 | bytes 12507136 | tf_op jit(solution)/shard_map/sub | solution.py:90
  110.2 1.8 constant_dynamic-update-slice_fusion.2
  114.3 2.3 copy-done.2
  116.7 1.7 collective-permute-start.9
  121.9 1.8 slice_bitcast_fusion.24
  123.7 1.5 maximum_bitcast_fusion.7
  127.0 1.3 pad_maximum_fusion.5
  128.3 5.1 %collective-permute-start.11 = (f32[19,34,1,128]{3,2,1,0:T(1,128)}, f32[19,34,1,128]{3,2,1,0:T(1,128)}, u32[]{:S(2)}, u32[]{:S(2)}) collective-permute-start(f32[19,34,1,128]{3,2,1,0:T(1,128)} %get-tuple-element.146), channel_id=1, source_target_pairs={{1,0},{2,1},{3,2},{4,3},{5,4},{6,5},{7,6},{0,7},{9,8},{10,9},{11,1... | collective-permute-start | bytes 992264 | tf_op jit(solution)/shard_map/ppermute | solution.py:45
  139.7 3.3 collective-permute-done.10
  142.9 3.3 collective-permute-done.11
  146.2 1.3 maximum_bitcast_fusion.5
  151.4 3.6 multiply_subtract_fusion
  156.7 1.2 copy.489
  157.9 1.1 copy.495
  161.0 4.1 %constant_dynamic-update-slice_fusion.12 = (f32[19,32,16,128]{3,2,1,0:T(8,128)S(1)}, f32[1,32,16,128]{3,2,1,0:T(8,128)}, f32[1,32,16,128]{3,2,1,0:T(8,128)S(1)},...) fusion(f32[1,32,16,128]{3,2,1,0:T(8,128)} %get-tuple-element.70, ...), kind=kLoop, calls=%fused_computation.1082 | loop fusion | flops 5373951 | bytes 8912896
  165.1 2.3 copy.593
  170.4 2.2 copy-done
  172.8 1.7 collective-permute-start.13
  178.0 4.0 %pad_maximum_fusion.2 = (f32[19,34,1,128]{3,2,1,0:T(1,128)}, f32[19,34,1,128]{3,2,1,0:T(1,128)S(1)}) fusion(f32[19,1,16,128]{3,2,1,0:T(8,128)S(1)} %collective-permute-done.13, f32[19,32,16,128]{3,2,1,0:T(8,128)} %copy-done, f32[19,1,16,128]{3,2,1,0:T(8,128)S(1)} %collective-permute-done.12), kind=kLoop, calls=%fused_computation.81 | loop fusion | flops 330752 | bytes 5953536 | tf_op jit(solution)/shard_map/slice | solution.py:42
  182.0 4.9 %collective-permute-start.15 = (f32[19,34,1,128]{3,2,1,0:T(1,128)S(1)}, f32[19,34,1,128]{3,2,1,0:T(1,128)S(1)}, u32[]{:S(2)}, u32[]{:S(2)}) collective-permute-start(f32[19,34,1,128]{3,2,1,0:T(1,128)S(1)} %get-tuple-element.142), channel_id=1, source_target_pairs={{1,0},{2,1},{3,2},{4,3},{5,4},{6,5},{7,6},{0,7},{9,8},{10,9},{11,1... | collective-permute-start | bytes 992264 | tf_op jit(solution)/shard_map/ppermute | solution.py:45
  193.0 4.5 %collective-permute-done.14 = f32[19,34,1,128]{3,2,1,0:T(1,128)S(1)} collective-permute-done((f32[19,34,1,128]{3,2,1,0:T(1,128)}, f32[19,34,1,128]{3,2,1,0:T(1,128)S(1)}, u32[]{:S(2)}, u32[]{:S(2)}) %collective-permute-start.14) | collective-permute-done | bytes 330784 | tf_op jit(solution)/shard_map/ppermute | solution.py:44
  197.5 2.6 collective-permute-done.15
  200.1 1.5 maximum_bitcast_fusion.1
  206.2 1.9 fusion.506
  210.7 1.1 copy.509
  212.6 1.7 constant_dynamic-update-slice_fusion.11
  218.9 3.7 add_divide_fusion.3
  229.6 1.7 collective-permute-start.17
  231.5 1.4 collective-permute-done.16
  233.0 2.0 collective-permute-start.18
  235.4 2.3 collective-permute-done.18
  237.7 4.4 %collective-permute-done.19 = f32[3,34,1,128]{3,2,1,0:T(1,128)S(1)} collective-permute-done((f32[3,34,1,128]{3,2,1,0:T(1,128)S(1)}, f32[3,34,1,128]{3,2,1,0:T(1,128)S(1)}, u32[]{:S(2)}, u32[]{:S(2)}) %collective-permute-start.19) | collective-permute-done | bytes 52256 | tf_op jit(solution)/shard_map/ppermute | solution.py:44
  242.1 1.2 fusion.451
  249.2 1.8 bitcast_dynamic-update-slice_fusion.5
  252.7 27.3 %all-gather.2.cloned.1.call-done = bf16[32,128,128]{2,1,0:T(8,128)(2,1)} async-done(((bf16[32,16,128]{2,1,0:T(8,128)(2,1)}), bf16[32,128,128]{2,1,0:T(8,128)(2,1)}) %all-gather.2.cloned.1.call-update) | async-done | bytes 1048592 | tf_op jit(solution)/shard_map/all_gather | solution.py:206
  280.0 15.4 %fusion.634 = f32[32,128,128]{2,1,0:T(8,128)S(1)} fusion(f32[]{:T(128)} %bitcast.196, f32[]{:T(128)} %bitcast.194, f32[]{:T(128)} %bitcast.192, f32[]{:T(128)} %bitcast.190, f32[]{:T(128)} %bitcast.188, f32[]{:T(128)} %bitcast.186, f32[]{:T(128)} %bitcast.184, f32[]{:T(128)} %bitcast.182, f32[]{:T(128)} %bitcast.183, f32[]{:T(128)} %bitcast.185, ...), kind=kOutput, calls=%fused_computation.1069 | output fusion | flops 42991616 | bytes 3145792 | tf_op jit(solution)/shard_map/while/body/eval_jaxpr/jit(cumsum)/reduce_window_sum | solution.py:139
  295.5 21.1 %multiply_reduce_fusion.2 = f32[128,128]{1,0:T(8,128)S(1)} fusion(f32[]{:T(128)} %bitcast.206, f32[]{:T(128)} %bitcast.205, f32[]{:T(128)} %bitcast.204, f32[]{:T(128)} %bitcast.203, f32[]{:T(128)} %bitcast.202, f32[]{:T(128)} %bitcast.201, f32[]{:T(128)} %bitcast.200, f32[]{:T(128)} %bitcast.199, f32[32,128,128]{2,1,0:T(8,128)S(1)} %fusion.634, ...), kind=kLoop, calls=%fused_computation.4 | loop fusion | flops 39305216 | bytes 3276897 | tf_op jit(solution)/shard_map/while/body/eval_jaxpr/reduce_sum | solution.py:143
  316.6 21.0 %multiply_reduce_fusion.1 = f32[128,128]{1,0:T(8,128)S(1)} fusion(f32[]{:T(128)} %bitcast.215, f32[]{:T(128)} %bitcast.214, f32[]{:T(128)} %bitcast.213, f32[]{:T(128)} %bitcast.212, f32[]{:T(128)} %bitcast.211, f32[]{:T(128)} %bitcast.210, f32[]{:T(128)} %bitcast.209, f32[]{:T(128)} %bitcast.208, f32[32,128,128]{2,1,0:T(8,128)S(1)} %fusion.634, ...), kind=kLoop, calls=%fused_computation.3 | loop fusion | flops 39305216 | bytes 3276897 | tf_op jit(solution)/shard_map/while/body/eval_jaxpr/reduce_sum | solution.py:143
  337.6 20.6 %multiply_reduce_fusion = f32[128,128]{1,0:T(8,128)S(1)} fusion(f32[]{:T(128)} %bitcast.224, f32[]{:T(128)} %bitcast.223, f32[]{:T(128)} %bitcast.222, f32[]{:T(128)} %bitcast.221, f32[]{:T(128)} %bitcast.220, f32[]{:T(128)} %bitcast.219, f32[]{:T(128)} %bitcast.218, f32[]{:T(128)} %bitcast.217, f32[32,128,128]{2,1,0:T(8,128)S(1)} %fusion.634, ...), kind=kLoop, calls=%fused_computation.2 | loop fusion | flops 39305216 | bytes 3276897 | tf_op jit(solution)/shard_map/while/body/eval_jaxpr/reduce_sum | solution.py:143
  361.0 1.7 collective-permute-start.21
  363.5 1.9 collective-permute-done.21
  (602 shorter events, 103.4 us)
Async XLA Ops:
  7.2 272.9 %all-gather.2.cloned.1.call-start = ((), (), s32[]{:S(2)}) async-start(), calls=%async_computation | async-start | bytes 1179648 | tf_op jit(solution)/shard_map/all_gather | solution.py:206
  13.3 6.7 %collective-permute-start = (f32[19,1,16,128]{3,2,1,0:T(8,128)S(1)}, f32[19,1,16,128]{3,2,1,0:T(8,128)S(1)}, u32[]{:S(2)}, u32[]{:S(2)}) collective-permute-start(f32[19,1,16,128]{3,2,1,0:T(8,128)S(1)} %get-tuple-element.183), channel_id=1, source_target_pairs={{0,8},{8,16},{16,24},{24,0},{1,9},{9,17},{17,25},{25,1},{2,10},{10... | collective-permute-start | bytes 466952 | tf_op jit(solution)/shard_map/ppermute | solution.py:44
  13.9 6.3 %collective-permute-start.1 = (f32[19,1,16,128]{3,2,1,0:T(8,128)S(1)}, f32[19,1,16,128]{3,2,1,0:T(8,128)S(1)}, u32[]{:S(2)}, u32[]{:S(2)}) collective-permute-start(f32[19,1,16,128]{3,2,1,0:T(8,128)S(1)} %get-tuple-element.184), channel_id=1, source_target_pairs={{8,0},{16,8},{24,16},{0,24},{9,1},{17,9},{25,17},{1,25},{10,2},{18... | collective-permute-start | bytes 466952 | tf_op jit(solution)/shard_map/ppermute | solution.py:45
  16.7 7.5 %copy-start.73 = (f32[32,16,1]{2,1,0:T(8,128)}, f32[32,16,1]{2,1,0:T(8,128)S(1)}, u32[]{:S(2)}) copy-start(f32[32,16,1]{2,1,0:T(8,128)S(1)} %slice.1217) | copy-start | bytes 6148
  20.1 9.5 %copy-start.5 = (f32[19,32,16,128]{3,2,1,0:T(8,128)S(1)}, f32[19,32,16,128]{3,2,1,0:T(8,128)}, u32[]{:S(2)}) copy-start(f32[19,32,16,128]{3,2,1,0:T(8,128)} %copy-done.4) | copy-start | bytes 14942212
  24.2 17.1 %collective-permute-start.2 = (f32[19,34,1,128]{3,2,1,0:T(1,128)}, f32[19,34,1,128]{3,2,1,0:T(1,128)S(1)}, u32[]{:S(2)}, u32[]{:S(2)}) collective-permute-start(f32[19,34,1,128]{3,2,1,0:T(1,128)} %get-tuple-element.153), channel_id=1, source_target_pairs={{0,1},{1,2},{2,3},{3,4},{4,5},{5,6},{6,7},{7,0},{8,9},{9,10},{10,1... | collective-permute-start | bytes 992264 | tf_op jit(solution)/shard_map/ppermute | solution.py:44
  26.3 17.3 %collective-permute-start.3 = (f32[19,34,1,128]{3,2,1,0:T(1,128)}, f32[19,34,1,128]{3,2,1,0:T(1,128)S(1)}, u32[]{:S(2)}, u32[]{:S(2)}) collective-permute-start(f32[19,34,1,128]{3,2,1,0:T(1,128)} %get-tuple-element.154), channel_id=1, source_target_pairs={{1,0},{2,1},{3,2},{4,3},{5,4},{6,5},{7,6},{0,7},{9,8},{10,9},{11,1... | collective-permute-start | bytes 992264 | tf_op jit(solution)/shard_map/ppermute | solution.py:45
  30.8 5.6 %copy-start.80 = (f32[32,16,1]{2,1,0:T(8,128)}, f32[32,16,1]{2,1,0:T(8,128)S(1)}, u32[]{:S(2)}) copy-start(f32[32,16,1]{2,1,0:T(8,128)S(1)} %slice.1221) | copy-start | bytes 6148
  30.9 14.1 %copy-start.83 = (f32[32,16,1]{2,1,0:T(8,128)}, f32[32,16,1]{2,1,0:T(8,128)S(1)}, u32[]{:S(2)}) copy-start(f32[32,16,1]{2,1,0:T(8,128)S(1)} %slice.1227) | copy-start | bytes 6148
  48.2 5.3 %copy-start.92 = (f32[32,16,127]{2,1,0:T(8,128)S(1)}, f32[32,16,127]{2,1,0:T(8,128)}, u32[]{:S(2)}) copy-start(f32[32,16,127]{2,1,0:T(8,128)} %get-tuple-element.284) | copy-start | bytes 780292
  67.3 5.0 %collective-permute-start.4 = (f32[19,1,16,128]{3,2,1,0:T(8,128)S(1)}, f32[19,1,16,128]{3,2,1,0:T(8,128)S(1)}, u32[]{:S(2)}, u32[]{:S(2)}) collective-permute-start(f32[19,1,16,128]{3,2,1,0:T(8,128)S(1)} %get-tuple-element.179), channel_id=1, source_target_pairs={{0,8},{8,16},{16,24},{24,0},{1,9},{9,17},{17,25},{25,1},{2,10},{10... | collective-permute-start | bytes 466952 | tf_op jit(solution)/shard_map/ppermute | solution.py:44
  67.3 5.3 %collective-permute-start.5 = (f32[19,1,16,128]{3,2,1,0:T(8,128)S(1)}, f32[19,1,16,128]{3,2,1,0:T(8,128)S(1)}, u32[]{:S(2)}, u32[]{:S(2)}) collective-permute-start(f32[19,1,16,128]{3,2,1,0:T(8,128)S(1)} %get-tuple-element.180), channel_id=1, source_target_pairs={{8,0},{16,8},{24,16},{0,24},{9,1},{17,9},{25,17},{1,25},{10,2},{18... | collective-permute-start | bytes 466952 | tf_op jit(solution)/shard_map/ppermute | solution.py:45
  70.5 5.5 %slice-start.6 = ((s8[4980736]{0:T(1024)(128)(4,1)}), s8[786432]{0:T(1024)(128)(4,1)S(1)}, s32[]{:S(2)}) async-start(s8[4980736]{0:T(1024)(128)(4,1)} %bitcast.1163), calls=%async_computation.7 | async-start | bytes 1572864
  77.3 15.6 %collective-permute-start.6 = (f32[19,34,1,128]{3,2,1,0:T(1,128)}, f32[19,34,1,128]{3,2,1,0:T(1,128)}, u32[]{:S(2)}, u32[]{:S(2)}) collective-permute-start(f32[19,34,1,128]{3,2,1,0:T(1,128)} %get-tuple-element.149), channel_id=1, source_target_pairs={{0,1},{1,2},{2,3},{3,4},{4,5},{5,6},{6,7},{7,0},{8,9},{9,10},{10,1... | collective-permute-start | bytes 992264 | tf_op jit(solution)/shard_map/ppermute | solution.py:44
  77.6 18.3 %collective-permute-start.7 = (f32[19,34,1,128]{3,2,1,0:T(1,128)}, f32[19,34,1,128]{3,2,1,0:T(1,128)}, u32[]{:S(2)}, u32[]{:S(2)}) collective-permute-start(f32[19,34,1,128]{3,2,1,0:T(1,128)} %get-tuple-element.150), channel_id=1, source_target_pairs={{1,0},{2,1},{3,2},{4,3},{5,4},{6,5},{7,6},{0,7},{9,8},{10,9},{11,1... | collective-permute-start | bytes 992264 | tf_op jit(solution)/shard_map/ppermute | solution.py:45
  83.3 9.7 %copy-start.78 = (f32[32,16,1]{2,1,0:T(8,128)}, f32[32,16,1]{2,1,0:T(8,128)S(1)}, u32[]{:S(2)}) copy-start(f32[32,16,1]{2,1,0:T(8,128)S(1)} %slice.1249) | copy-start | bytes 6148
  83.4 9.5 %copy-start.79 = (f32[32,16,1]{2,1,0:T(8,128)}, f32[32,16,1]{2,1,0:T(8,128)S(1)}, u32[]{:S(2)}) copy-start(f32[32,16,1]{2,1,0:T(8,128)S(1)} %slice.1243) | copy-start | bytes 6148
  99.3 6.2 %copy-start.89 = (f32[32,16,1]{2,1,0:T(8,128)}, f32[32,16,1]{2,1,0:T(8,128)S(1)}, u32[]{:S(2)}) copy-start(f32[32,16,1]{2,1,0:T(8,128)S(1)} %slice.1257) | copy-start | bytes 6148
  109.9 8.5 %copy-start.54 = (f32[32,16,128]{2,1,0:T(8,128)}, f32[32,16,128]{2,1,0:T(8,128)S(1)}, u32[]{:S(2)}) copy-start(f32[32,16,128]{2,1,0:T(8,128)S(1)} %get-tuple-element.58) | copy-start | bytes 786436
  109.9 8.5 %copy-start.56 = (f32[32,16,128]{2,1,0:T(8,128)}, f32[32,16,128]{2,1,0:T(8,128)S(1)}, u32[]{:S(2)}) copy-start(f32[32,16,128]{2,1,0:T(8,128)S(1)} %get-tuple-element.59) | copy-start | bytes 786436
  109.9 9.6 %copy-start.65 = (f32[32,16,128]{2,1,0:T(8,128)}, f32[32,16,128]{2,1,0:T(8,128)S(1)}, u32[]{:S(2)}) copy-start(f32[32,16,128]{2,1,0:T(8,128)S(1)} %get-tuple-element.57) | copy-start | bytes 786436
  116.6 7.0 %collective-permute-start.8 = (f32[19,1,16,128]{3,2,1,0:T(8,128)S(1)}, f32[19,1,16,128]{3,2,1,0:T(8,128)S(1)}, u32[]{:S(2)}, u32[]{:S(2)}) collective-permute-start(f32[19,1,16,128]{3,2,1,0:T(8,128)S(1)} %get-tuple-element.175), channel_id=1, source_target_pairs={{0,8},{8,16},{16,24},{24,0},{1,9},{9,17},{17,25},{25,1},{2,10},{10... | collective-permute-start | bytes 466952 | tf_op jit(solution)/shard_map/ppermute | solution.py:44
  116.7 7.0 %collective-permute-start.9 = (f32[19,1,16,128]{3,2,1,0:T(8,128)S(1)}, f32[19,1,16,128]{3,2,1,0:T(8,128)S(1)}, u32[]{:S(2)}, u32[]{:S(2)}) collective-permute-start(f32[19,1,16,128]{3,2,1,0:T(8,128)S(1)} %get-tuple-element.176), channel_id=1, source_target_pairs={{8,0},{16,8},{24,16},{0,24},{9,1},{17,9},{25,17},{1,25},{10,2},{18... | collective-permute-start | bytes 466952 | tf_op jit(solution)/shard_map/ppermute | solution.py:45
  121.0 6.0 %slice-start.2 = ((s8[4980736]{0:T(1024)(128)(4,1)}), s8[786432]{0:T(1024)(128)(4,1)S(1)}, s32[]{:S(2)}) async-start(s8[4980736]{0:T(1024)(128)(4,1)} %bitcast.1159), calls=%async_computation.3 | async-start | bytes 1572864
  125.2 9.2 %copy-start.104 = (f32[32,16,128]{2,1,0:T(8,128)}, f32[32,16,128]{2,1,0:T(8,128)S(1)}, u32[]{:S(2)}) copy-start(f32[32,16,128]{2,1,0:T(8,128)S(1)} %get-tuple-element.158) | copy-start | bytes 786436
  128.3 14.6 %collective-permute-start.10 = (f32[19,34,1,128]{3,2,1,0:T(1,128)}, f32[19,34,1,128]{3,2,1,0:T(1,128)S(1)}, u32[]{:S(2)}, u32[]{:S(2)}) collective-permute-start(f32[19,34,1,128]{3,2,1,0:T(1,128)} %get-tuple-element.145), channel_id=1, source_target_pairs={{0,1},{1,2},{2,3},{3,4},{4,5},{5,6},{6,7},{7,0},{8,9},{9,10},{10,1... | collective-permute-start | bytes 992264 | tf_op jit(solution)/shard_map/ppermute | solution.py:44
  128.3 17.9 %collective-permute-start.11 = (f32[19,34,1,128]{3,2,1,0:T(1,128)}, f32[19,34,1,128]{3,2,1,0:T(1,128)}, u32[]{:S(2)}, u32[]{:S(2)}) collective-permute-start(f32[19,34,1,128]{3,2,1,0:T(1,128)} %get-tuple-element.146), channel_id=1, source_target_pairs={{1,0},{2,1},{3,2},{4,3},{5,4},{6,5},{7,6},{0,7},{9,8},{10,9},{11,1... | collective-permute-start | bytes 992264 | tf_op jit(solution)/shard_map/ppermute | solution.py:45
  134.4 8.5 %copy-start.81 = (f32[32,16,1]{2,1,0:T(8,128)}, f32[32,16,1]{2,1,0:T(8,128)S(1)}, u32[]{:S(2)}) copy-start(f32[32,16,1]{2,1,0:T(8,128)S(1)} %slice.1271) | copy-start | bytes 6148
  134.6 8.3 %copy-start.84 = (f32[32,16,1]{2,1,0:T(8,128)}, f32[32,16,1]{2,1,0:T(8,128)S(1)}, u32[]{:S(2)}) copy-start(f32[32,16,1]{2,1,0:T(8,128)S(1)} %slice.1265) | copy-start | bytes 6148
  138.9 12.4 %slice-start.4 = ((s8[4980736]{0:T(1024)(128)(4,1)}), s8[4194304]{0:T(1024)(128)(4,1)S(1)}, s32[]{:S(2)}) async-start(s8[4980736]{0:T(1024)(128)(4,1)} %bitcast.1161), calls=%async_computation.5 | async-start | bytes 8388608
  139.7 11.6 %slice-start.5 = ((s8[4980736]{0:T(1024)(128)(4,1)}), s8[786432]{0:T(1024)(128)(4,1)S(1)}, s32[]{:S(2)}) async-start(s8[4980736]{0:T(1024)(128)(4,1)} %bitcast.1161), calls=%async_computation.6 | async-start | bytes 1572864
  148.5 6.4 %copy-start.86 = (f32[32,16,1]{2,1,0:T(8,128)}, f32[32,16,1]{2,1,0:T(8,128)S(1)}, u32[]{:S(2)}) copy-start(f32[32,16,1]{2,1,0:T(8,128)S(1)} %slice.1273) | copy-start | bytes 6148
  149.5 5.5 %copy-start.87 = (f32[32,16,1]{2,1,0:T(8,128)}, f32[32,16,1]{2,1,0:T(8,128)S(1)}, u32[]{:S(2)}) copy-start(f32[32,16,1]{2,1,0:T(8,128)S(1)} %slice.1279) | copy-start | bytes 6148
  156.7 17.8 %copy-start.7 = (f32[32,16,1]{2,1,0:T(8,128)}, f32[32,16,1]{2,1,0:T(8,128)S(1)}, u32[]{:S(2)}) copy-start(f32[32,16,1]{2,1,0:T(8,128)S(1)} %slice.1283) | copy-start | bytes 6148
  172.7 5.3 %collective-permute-start.12 = (f32[19,1,16,128]{3,2,1,0:T(8,128)S(1)}, f32[19,1,16,128]{3,2,1,0:T(8,128)S(1)}, u32[]{:S(2)}, u32[]{:S(2)}) collective-permute-start(f32[19,1,16,128]{3,2,1,0:T(8,128)S(1)} %get-tuple-element.171), channel_id=1, source_target_pairs={{0,8},{8,16},{16,24},{24,0},{1,9},{9,17},{17,25},{25,1},{2,10},{10... | collective-permute-start | bytes 466952 | tf_op jit(solution)/shard_map/ppermute | solution.py:44
  172.8 5.2 %collective-permute-start.13 = (f32[19,1,16,128]{3,2,1,0:T(8,128)S(1)}, f32[19,1,16,128]{3,2,1,0:T(8,128)S(1)}, u32[]{:S(2)}, u32[]{:S(2)}) collective-permute-start(f32[19,1,16,128]{3,2,1,0:T(8,128)S(1)} %get-tuple-element.172), channel_id=1, source_target_pairs={{8,0},{16,8},{24,16},{0,24},{9,1},{17,9},{25,17},{1,25},{10,2},{18... | collective-permute-start | bytes 466952 | tf_op jit(solution)/shard_map/ppermute | solution.py:45
  177.6 9.2 %copy-start.1 = (f32[19,32,16,128]{3,2,1,0:T(8,128)S(1)}, f32[19,32,16,128]{3,2,1,0:T(8,128)}, u32[]{:S(2)}) copy-start(f32[19,32,16,128]{3,2,1,0:T(8,128)} %copy-done) | copy-start | bytes 14942212
  178.0 22.1 %copy-start.49 = (f32[19,1,16,128]{3,2,1,0:T(8,128)}, f32[19,1,16,128]{3,2,1,0:T(8,128)S(1)}, u32[]{:S(2)}) copy-start(f32[19,1,16,128]{3,2,1,0:T(8,128)S(1)} %collective-permute-done.12) | copy-start | bytes 466948
  178.0 22.1 %copy-start.51 = (f32[19,1,16,128]{3,2,1,0:T(8,128)}, f32[19,1,16,128]{3,2,1,0:T(8,128)S(1)}, u32[]{:S(2)}) copy-start(f32[19,1,16,128]{3,2,1,0:T(8,128)S(1)} %collective-permute-done.13) | copy-start | bytes 466948
  182.0 15.6 %collective-permute-start.14 = (f32[19,34,1,128]{3,2,1,0:T(1,128)}, f32[19,34,1,128]{3,2,1,0:T(1,128)S(1)}, u32[]{:S(2)}, u32[]{:S(2)}) collective-permute-start(f32[19,34,1,128]{3,2,1,0:T(1,128)} %get-tuple-element.141), channel_id=1, source_target_pairs={{0,1},{1,2},{2,3},{3,4},{4,5},{5,6},{6,7},{7,0},{8,9},{9,10},{10,1... | collective-permute-start | bytes 992264 | tf_op jit(solution)/shard_map/ppermute | solution.py:44
  182.0 18.1 %collective-permute-start.15 = (f32[19,34,1,128]{3,2,1,0:T(1,128)S(1)}, f32[19,34,1,128]{3,2,1,0:T(1,128)S(1)}, u32[]{:S(2)}, u32[]{:S(2)}) collective-permute-start(f32[19,34,1,128]{3,2,1,0:T(1,128)S(1)} %get-tuple-element.142), channel_id=1, source_target_pairs={{1,0},{2,1},{3,2},{4,3},{5,4},{6,5},{7,6},{0,7},{9,8},{10,9},{11,1... | collective-permute-start | bytes 992264 | tf_op jit(solution)/shard_map/ppermute | solution.py:45
  192.3 13.8 %slice-start = ((s8[4980736]{0:T(1024)(128)(4,1)}), s8[4194304]{0:T(1024)(128)(4,1)S(1)}, s32[]{:S(2)}) async-start(s8[4980736]{0:T(1024)(128)(4,1)} %bitcast.1157), calls=%async_computation.1 | async-start | bytes 8388608
  193.0 15.0 %copy-start.27 = (f32[32,16,127]{2,1,0:T(8,128)}, f32[32,16,127]{2,1,0:T(8,128)S(1)}, u32[]{:S(2)}) copy-start(f32[32,16,127]{2,1,0:T(8,128)S(1)} %get-tuple-element.224) | copy-start | bytes 780292
  193.0 13.1 %slice-start.1 = ((s8[4980736]{0:T(1024)(128)(4,1)}), s8[786432]{0:T(1024)(128)(4,1)S(1)}, s32[]{:S(2)}) async-start(s8[4980736]{0:T(1024)(128)(4,1)} %bitcast.1157), calls=%async_computation.2 | async-start | bytes 1572864
  202.4 5.7 %copy-start.31 = (f32[32,16,127]{2,1,0:T(8,128)}, f32[32,16,127]{2,1,0:T(8,128)S(1)}, u32[]{:S(2)}) copy-start(f32[32,16,127]{2,1,0:T(8,128)S(1)} %get-tuple-element.210) | copy-start | bytes 780292
  202.6 5.4 %copy-start.10 = (f32[32,16,1]{2,1,0:T(8,128)}, f32[32,16,1]{2,1,0:T(8,128)S(1)}, u32[]{:S(2)}) copy-start(f32[32,16,1]{2,1,0:T(8,128)S(1)} %slice.1295) | copy-start | bytes 6148
  229.6 12.5 %copy-start.148 = (f32[32,16,1]{2,1,0:T(8,128)S(1)}, f32[32,16,1]{2,1,0:T(8,128)}, u32[]{:S(2)}) copy-start(f32[32,16,1]{2,1,0:T(8,128)} %get-tuple-element.199) | copy-start | bytes 6148
  229.6 12.5 %copy-start.149 = (f32[32,16,1]{2,1,0:T(8,128)S(1)}, f32[32,16,1]{2,1,0:T(8,128)}, u32[]{:S(2)}) copy-start(f32[32,16,1]{2,1,0:T(8,128)} %get-tuple-element.200) | copy-start | bytes 6148
  229.6 12.5 %copy-start.150 = (f32[32,16,127]{2,1,0:T(8,128)S(1)}, f32[32,16,127]{2,1,0:T(8,128)}, u32[]{:S(2)}) copy-start(f32[32,16,127]{2,1,0:T(8,128)} %get-tuple-element.201) | copy-start | bytes 780292
  229.6 12.5 %copy-start.151 = (f32[32,16,127]{2,1,0:T(8,128)S(1)}, f32[32,16,127]{2,1,0:T(8,128)}, u32[]{:S(2)}) copy-start(f32[32,16,127]{2,1,0:T(8,128)} %get-tuple-element.202) | copy-start | bytes 780292
  229.6 3.3 collective-permute-start.16
  229.6 3.3 collective-permute-start.17
  233.0 4.7 %collective-permute-start.18 = (f32[3,34,1,128]{3,2,1,0:T(1,128)S(1)}, f32[3,34,1,128]{3,2,1,0:T(1,128)S(1)}, u32[]{:S(2)}, u32[]{:S(2)}) collective-permute-start(f32[3,34,1,128]{3,2,1,0:T(1,128)S(1)} %get-tuple-element.187), channel_id=1, source_target_pairs={{1,0},{2,1},{3,2},{4,3},{5,4},{6,5},{7,6},{0,7},{9,8},{10,9},{11,1... | collective-permute-start | bytes 156680 | tf_op jit(solution)/shard_map/ppermute | solution.py:45
  235.0 8.3 %copy-start.152 = (f32[1,5,8]{2,0,1:T(1,128)S(1)}, f32[1,5,8]{2,0,1:T(1,128)}, u32[]{:S(2)}) copy-start(f32[1,5,8]{2,0,1:T(1,128)} %param.6) | copy-start | bytes 484
  235.0 9.1 %copy-start.153 = (s32[4]{0:T(128)S(1)}, s32[4]{0:T(128)}, u32[]{:S(2)}) copy-start(s32[4]{0:T(128)} %constant.103) | copy-start | bytes 52
  235.0 7.1 %collective-permute-start.19 = (f32[3,34,1,128]{3,2,1,0:T(1,128)S(1)}, f32[3,34,1,128]{3,2,1,0:T(1,128)S(1)}, u32[]{:S(2)}, u32[]{:S(2)}) collective-permute-start(f32[3,34,1,128]{3,2,1,0:T(1,128)S(1)} %get-tuple-element.188), channel_id=1, source_target_pairs={{0,1},{1,2},{2,3},{3,4},{4,5},{5,6},{6,7},{7,0},{8,9},{9,10},{10,1... | collective-permute-start | bytes 156680 | tf_op jit(solution)/shard_map/ppermute | solution.py:44
  242.1 5.5 %copy-start.26 = (f32[32,16,127]{2,1,0:T(8,128)S(1)}, f32[32,16,127]{2,1,0:T(8,128)}, u32[]{:S(2)}) copy-start(f32[32,16,127]{2,1,0:T(8,128)} %get-tuple-element.218) | copy-start | bytes 780292
  242.1 6.3 %copy-start.24 = (f32[32,16,127]{2,1,0:T(8,128)S(1)}, f32[32,16,127]{2,1,0:T(8,128)}, u32[]{:S(2)}) copy-start(f32[32,16,127]{2,1,0:T(8,128)} %get-tuple-element.220) | copy-start | bytes 780292
  243.3 7.8 %copy-start.28 = (f32[32,16,127]{2,1,0:T(8,128)S(1)}, f32[32,16,127]{2,1,0:T(8,128)}, u32[]{:S(2)}) copy-start(f32[32,16,127]{2,1,0:T(8,128)} %copy-done.27) | copy-start | bytes 780292
  246.1 5.8 %copy-start.11 = (f32[32,16,1]{2,1,0:T(8,128)S(1)}, f32[32,16,1]{2,1,0:T(8,128)}, u32[]{:S(2)}) copy-start(f32[32,16,1]{2,1,0:T(8,128)} %copy-done.10) | copy-start | bytes 6148
  246.1 5.8 %copy-start.32 = (f32[32,16,127]{2,1,0:T(8,128)S(1)}, f32[32,16,127]{2,1,0:T(8,128)}, u32[]{:S(2)}) copy-start(f32[32,16,127]{2,1,0:T(8,128)} %copy-done.31) | copy-start | bytes 780292
  280.0 15.5 %copy-start.154 = (bf16[32,128,128]{2,1,0:T(8,128)(2,1)S(1)}, bf16[32,128,128]{2,1,0:T(8,128)(2,1)}, u32[]{:S(2)}) copy-start(bf16[32,128,128]{2,1,0:T(8,128)(2,1)} %all-gather.2.cloned.1.call-done) | copy-start | bytes 3145732
  359.0 2.0 collective-permute-start.20
  361.0 4.4 %collective-permute-start.21 = (f32[1,4,32,128]{3,2,1,0:T(8,128)S(1)}, f32[1,4,32,128]{3,2,1,0:T(8,128)S(1)}, u32[]{:S(2)}, u32[]{:S(2)}) collective-permute-start(f32[1,4,32,128]{3,2,1,0:T(8,128)S(1)} %get-tuple-element.288), channel_id=1, source_target_pairs={{0,16},{16,0},{8,24},{24,8},{1,17},{17,1},{9,25},{25,9},{2,18},{18... | collective-permute-start | bytes 196616 | tf_op jit(solution)/shard_map/ppermute | solution.py:57
  (122 other events, 436.5 us)
Sparse Core Ops, SparseCore 0:
  243.4 36.5 all-gather.1
where the time goes:
time: 379 us; the launch traced here: 373 us
  other arithmetic  154 us (41%)
  local copies, waits for them, and re-layouts  101 us (27%)
  waiting for transfers between devices  66.1 us (17%)
  starting transfers between devices  34 us (9%)
  between operations  17.6 us (5%)
    concatenate x75, local copies, waits for them, and re-layouts, stream(): window = jnp.roll(window, shift_z, axis=2)  65.2 us
    reduce_sum x3, other arithmetic, render_block(): jnp.sum(weight * emission[channel], axis=0)  62.7 us
    unnamed x85, other arithmetic  30.9 us
    ppermute x10, starting transfers between devices, with_halo(): after = lax.ppermute(first, axis, down)  28.8 us
    all_gather x1, waiting for transfers between devices, on_device(): lax.all_gather(vorticity, 'image', axis=1, tiled=True)  27.3 us
    ppermute x10, waiting for transfers between devices, with_halo(): before = lax.ppermute(last, axis, up)  23 us
    unnamed x335, local copies, waits for them, and re-layouts  18.2 us
    another operation x1, other arithmetic, render_block(): inclusive = jnp.cumsum(optical, axis=0)  15.4 us
  transfers between devices with their start and end apart: 23, of which 16 were waited for; matrix products, arithmetic and copies ran while one was open for 14% of the time, Pallas kernels for 0%

commit v1 on v0

v1 whole, which is shorter than its diff:
```python
import functools
import math

import jax
import jax.numpy as jnp
from jax import lax
from jax.experimental import pallas as pl
from jax.experimental.pallas import tpu as pltpu
from jax.sharding import PartitionSpec as P

STEPS = 4
MESH = pl.DeviceIdType.MESH

lattice_velocities = (
    (0, 0, 0),
    (1, 0, 0),
    (-1, 0, 0),
    (0, 1, 0),
    (0, -1, 0),
    (0, 0, 1),
    (0, 0, -1),
    (1, 1, 0),
    (-1, -1, 0),
    (1, -1, 0),
    (-1, 1, 0),
    (1, 0, 1),
    (-1, 0, -1),
    (1, 0, -1),
    (-1, 0, 1),
    (0, 1, 1),
    (0, -1, -1),
    (0, 1, -1),
    (0, -1, 1),
)
relaxation = 1.25
bump_width = 0.15
level_offset = 0.05
LOG2E = math.log2(math.e)
SCALE = math.sqrt(LOG2E) / bump_width

COUNT = len(lattice_velocities)
ORDER = (
    [n for n in range(COUNT) if lattice_velocities[n][0] == 1]
    + [n for n in range(COUNT) if lattice_velocities[n][0] == -1]
    + [n for n in range(COUNT) if lattice_velocities[n][0] == 0]
)
SLOT = {number: place for place, number in enumerate(ORDER)}
UP_Y = [n for n in range(COUNT) if lattice_velocities[n][1] == 1]
DOWN_Y = [n for n in range(COUNT) if lattice_velocities[n][1] == -1]
CROSS = len(UP_Y)
CORNERS = [n for n in range(COUNT) if lattice_velocities[n][0] and lattice_velocities[n][1]]
PAIRS = [(n, n + 1) for n in range(1, COUNT, 2)]
LOW = 8
ROWS = 8


def add_all(values):
    while len(values) > 1:
        paired = [a + b for a, b in zip(values[0::2], values[1::2])]
        values = paired + ([values[-1]] if len(values) % 2 else [])
    return values[0]


def moments(field):
    diffs = {}
    sums = [field[0]]
    for plus, minus in PAIRS:
        sums.append(field[plus] + field[minus])
        diffs[plus] = field[plus] - field[minus]
    momentum = []
    for axis in range(3):
        total = diffs[1 + 2 * axis]
        for plus, _ in PAIRS[3:]:
            factor = lattice_velocities[plus][axis]
            if factor == 1:
                total = total + diffs[plus]
            elif factor == -1:
                total = total - diffs[plus]
        momentum.append(total)
    return add_all(sums), momentum


def collide(field):
    density, momentum = moments(field)
    inverse = 1.0 / density
    square = momentum[0] * momentum[0] + momentum[1] * momentum[1] + momentum[2] * momentum[2]
    even = density - 1.5 * (square * inverse)
    keep = 1.0 - relaxation
    result = [keep * field[0] + (relaxation / 3.0) * even] + [None] * (COUNT - 1)
    parts = {}
    for divisor in (18.0, 36.0):
        parts[divisor] = ((relaxation / divisor) * even, (relaxation * 4.5 / divisor) * inverse)
    for plus, minus in PAIRS:
        project = None
        for axis in range(3):
            factor = lattice_velocities[plus][axis]
            if factor:
                if project is None:
                    project = momentum[axis]
                elif factor == 1:
                    project = project + momentum[axis]
                else:
                    project = project - momentum[axis]
        divisor = 18.0 if plus < 7 else 36.0
        base, curve = parts[divisor]
        symmetric = base + curve * (project * project)
        odd = (3.0 * relaxation / divisor) * project
        result[plus] = keep * field[plus] + (symmetric + odd)
        result[minus] = keep * field[minus] + (symmetric - odd)
    return result


def kernel(
    sizes,
    f_hbm,
    par,
    direct,
    fout,
    vort,
    img,
    F,
    A,
    B,
    SY,
    RY,
    SC,
    RC,
    U,
    VS,
    VR,
    L,
    PA,
    PS,
    PR,
    in_sem,
    out_sem,
    halo_s,
    halo_r,
    flow_s,
    flow_r,
    pa_s,
    pa_r,
    pr_s,
    pr_r,
):
    nd, ni, X, W, NZ, bumps = sizes
    d = lax.axis_index("depth")
    i = lax.axis_index("image")
    halves = W // ROWS
    ratio = ni // nd
    chunks = 4
    step_x = X // chunks

    loads = [
        pltpu.make_async_copy(
            f_hbm.at[:, pl.ds(c * step_x, step_x)],
            F.at[:, pl.ds(c * step_x, step_x)],
            in_sem.at[c],
        )
        for c in range(chunks)
    ]
    for copy in loads:
        copy.start()

    barrier = pltpu.get_barrier_semaphore()
    everyone = nd * ni
    me = d * ni + i

    def greet(offset, carry):
        other = lax.rem(me + offset, everyone)
        pl.semaphore_signal(
            barrier,
            inc=1,
            device_id={"depth": other // ni, "image": lax.rem(other, ni)},
            device_id_type=MESH,
        )
        return carry

    lax.fori_loop(1, everyone, greet, 0)

    ray = X * nd
    for k in range(bumps):
        for kind in range(5):
            factor = SCALE if kind == 0 else (LOG2E / ray if kind == 1 else 1.0)
            value = par[0, kind, k] * factor
            PA[i, pl.ds(kind * bumps + k, 1), :] = jnp.full((1, NZ), value, jnp.float32)
    PA[i, pl.ds(5 * bumps, 1), :] = jnp.full((1, NZ), direct[0].astype(jnp.float32), jnp.float32)

    def to(cx, cy):
        return {"depth": lax.rem(d + cx + nd, nd), "image": lax.rem(i + cy + ni, ni)}

    def remote(src, dst, send, recv, target):
        return pltpu.make_async_remote_copy(
            src_ref=src,
            dst_ref=dst,
            send_sem=send,
            recv_sem=recv,
            device_id=target,
            device_id_type=MESH,
        )

    def store(D, x, h, values):
        for number in range(COUNT):
            D[SLOT[number], x + 1, pl.ds(LOW + ROWS * h, ROWS), :] = values[number]
        if h == 0:
            for j, number in enumerate(DOWN_Y):
                SY[0, j, pl.ds(x, 1), :] = values[number][0:1]
        if h == halves - 1:
            for j, number in enumerate(UP_Y):
                SY[1, j, pl.ds(x, 1), :] = values[number][ROWS - 1 : ROWS]

    def streamed(S, x, h):
        field = []
        for number in range(COUNT):
            cx, cy, cz = lattice_velocities[number]
            value = S[SLOT[number], x + 1 - cx, pl.ds(LOW + ROWS * h - cy, ROWS), :]
            if cz:
                value = pltpu.roll(value, cz % NZ, 1)
            field.append(value)
        return field

    def exchange(D, turn):
        slot = turn % 2
        for k, number in enumerate(CORNERS):
            cx, cy, _ = lattice_velocities[number]
            group = UP_Y if cy == 1 else DOWN_Y
            edge = X - 1 if cx == 1 else 0
            SC[k, 0:1, :] = SY[1 if cy == 1 else 0, group.index(number), edge : edge + 1, :]
        inner = pl.ds(LOW, W)
        copies = []

        def add(src, dst, target):
            k = len(copies)
            copies.append(remote(src, dst, halo_s.at[turn, k], halo_r.at[turn, k], target))

        add(SY.at[1], RY.at[slot, 1], to(0, 1))
        add(SY.at[0], RY.at[slot, 0], to(0, -1))
        for k, number in enumerate(CORNERS):
            cx, cy, _ = lattice_velocities[number]
            add(SC.at[k], RC.at[slot, k], to(cx, cy))
        add(D.at[pl.ds(0, CROSS), X, inner], D.at[pl.ds(0, CROSS), 0, inner], to(1, 0))
        add(D.at[pl.ds(CROSS, CROSS), 1, inner], D.at[pl.ds(CROSS, CROSS), X + 1, inner], to(-1, 0))
        for copy in copies:
            copy.start()
        for copy in copies:
            copy.wait()

        def unpack(x, carry):
            for j, number in enumerate(UP_Y):
                D[SLOT[number], x + 1, pl.ds(LOW - 1, 1), :] = RY[slot, 1, j, pl.ds(x, 1), :]
            for j, number in enumerate(DOWN_Y):
                D[SLOT[number], x + 1, pl.ds(LOW + W, 1), :] = RY[slot, 0, j, pl.ds(x, 1), :]
            return carry

        lax.fori_loop(0, X, unpack, 0)
        for k, number in enumerate(CORNERS):
            cx, cy, _ = lattice_velocities[number]
            row = LOW - 1 if cy == 1 else LOW + W
            D[SLOT[number], 0 if cx == 1 else X + 1, row : row + 1, :] = RC[slot, k, 0:1, :]

    def first(x, carry):
        for h in range(halves):
            field = [F[number, x, pl.ds(ROWS * h, ROWS), :] for number in range(COUNT)]
            store(A, x, h, collide(field))
        return carry

    for c in range(chunks):
        loads[c].wait()
        lax.fori_loop(c * step_x, (c + 1) * step_x, first, 0)

    pl.semaphore_wait(barrier, everyone - 1)
    shares = [
        remote(PA.at[i], PA.at[i], pa_s.at[o], pa_r.at[o], to(0, o)) for o in range(1, ni)
    ]
    exchange(A, 0)
    for copy in shares:
        copy.start()

    source, target = A, B
    for turn in range(1, STEPS):

        def middle(x, carry, source=source, target=target):
            for h in range(halves):
                store(target, x, h, collide(streamed(source, x, h)))
            return carry

        lax.fori_loop(0, X, middle, 0)
        exchange(target, turn)
        source, target = target, source

    def last(x, carry):
        for h in range(halves):
            field = streamed(source, x, h)
            for number in range(COUNT):
                F[number, x, pl.ds(ROWS * h, ROWS), :] = field[number]
            density, momentum = moments(field)
            inverse = 1.0 / density
            flow = [part * inverse for part in momentum]
            for place, axis in enumerate((1, 2, 0)):
                U[place, x + 1, pl.ds(LOW + ROWS * h, ROWS), :] = flow[axis]
            if h == 0:
                VS[0, 0, pl.ds(x, 1), :] = flow[2][0:1]
                VS[0, 1, pl.ds(x, 1), :] = flow[0][0:1]
            if h == halves - 1:
                VS[1, 0, pl.ds(x, 1), :] = flow[2][ROWS - 1 : ROWS]
                VS[1, 1, pl.ds(x, 1), :] = flow[0][ROWS - 1 : ROWS]
        return carry

    lax.fori_loop(0, X, last, 0)
    inner = pl.ds(LOW, W)
    flows = [
        remote(VS.at[1], VR.at[1], flow_s.at[0], flow_r.at[0], to(0, 1)),
        remote(VS.at[0], VR.at[0], flow_s.at[1], flow_r.at[1], to(0, -1)),
        remote(
            U.at[pl.ds(0, 2), X, inner],
            U.at[pl.ds(0, 2), 0, inner],
            flow_s.at[2],
            flow_r.at[2],
            to(1, 0),
        ),
        remote(
            U.at[pl.ds(0, 2), 1, inner],
            U.at[pl.ds(0, 2), X + 1, inner],
            flow_s.at[3],
            flow_r.at[3],
            to(-1, 0),
        ),
    ]
    for copy in flows:
        copy.start()
    out = pltpu.make_async_copy(F, fout, out_sem)
    out.start()
    for copy in shares:
        copy.wait()
    for copy in flows:
        copy.wait()

    def flow_rows(x, carry):
        for place, j in ((1, 0), (2, 1)):
            U[place, x + 1, pl.ds(LOW - 1, 1), :] = VR[1, j, pl.ds(x, 1), :]
            U[place, x + 1, pl.ds(LOW + W, 1), :] = VR[0, j, pl.ds(x, 1), :]
        return carry

    lax.fori_loop(0, X, flow_rows, 0)

    def spin(x, carry):
        def across_x(place):
            return (U[place, x + 2, inner, :] - U[place, x, inner, :]) * 0.5

        def across_y(place):
            above = U[place, x + 1, pl.ds(LOW + 1, W), :]
            return (above - U[place, x + 1, pl.ds(LOW - 1, W), :]) * 0.5

        def across_z(place):
            value = U[place, x + 1, inner, :]
            return (pltpu.roll(value, NZ - 1, 1) - pltpu.roll(value, 1, 1)) * 0.5

        spin_x = across_y(1) - across_z(0)
        spin_y = across_z(2) - across_x(1)
        spin_z = across_x(0) - across_y(2)
        size = jnp.sqrt(spin_x * spin_x + spin_y * spin_y + spin_z * spin_z)
        rounded = size.astype(jnp.bfloat16)
        vort[x] = rounded
        value = rounded.astype(jnp.float32)
        L[x] = (value / (value + level_offset)) * SCALE
        return carry

    lax.fori_loop(0, X, spin, 0)

    owner = i // ratio
    mine = d * ratio + lax.rem(i, ratio)

    def row(m, r):
        return jnp.broadcast_to(PA[m, pl.ds(r, 1), :], (ROWS, NZ))

    def blend(backward, through, colors, local_through, local_colors):
        fade = jnp.where(backward, local_through, 1.0)
        lit = jnp.where(backward, 1.0, through)
        mixed = [color * fade + lit * local for color, local in zip(colors, local_colors)]
        return through * local_through, mixed

    def piece(o, m):
        return remote(
            PS.at[m],
            PR.at[mine],
            pr_s.at[o],
            pr_r.at[mine],
            {"depth": owner, "image": m},
        )

    def render(o, carry):
        m = lax.rem(i + 1 + o, ni)
        backward = row(m, 5 * bumps) > 0.5

        def along(x, state):
            new = []
            levels = [L[x, pl.ds(ROWS * h, ROWS), :] for h in range(halves)]
            totals = [[None] * 4 for h in range(halves)]
            for k in range(bumps):
                centre = row(m, k)
                gains = [row(m, (1 + j) * bumps + k) for j in range(4)]
                for h in range(halves):
                    offset = levels[h] - centre
                    bump = jnp.exp2(-(offset * offset))
                    for j in range(4):
                        term = gains[j] * bump
                        totals[h][j] = term if k == 0 else totals[h][j] + term
            for h in range(halves):
                through, colors = state[4 * h], state[4 * h + 1 : 4 * h + 4]
                local = jnp.exp2(-totals[h][0])
                alpha = 1.0 - local
                shades = [alpha * total for total in totals[h][1:]]
                through, colors = blend(backward, through, colors, local, shades)
                new += [through] + list(colors)
            return tuple(new)

        zero = jnp.zeros((ROWS, NZ), jnp.float32)
        start = (jnp.ones((ROWS, NZ), jnp.float32), zero, zero, zero) * halves
        state = lax.fori_loop(0, X, along, start)
        for h in range(halves):
            through, colors = state[4 * h], state[4 * h + 1 : 4 * h + 4]
            for j, value in enumerate(list(colors) + [through]):
                PS[m, j, pl.ds(ROWS * h, ROWS), :] = value
        local_target = jnp.logical_and(owner == d, m == i)

        @pl.when(local_target)
        def _():
            PR[mine] = PS[m]

        @pl.when(jnp.logical_not(local_target))
        def _():
            piece(o, m).start()

        return carry

    lax.fori_loop(0, ni, render, 0)

    def sent(o, carry):
        m = lax.rem(i + 1 + o, ni)

        @pl.when(jnp.logical_not(jnp.logical_and(owner == d, m == i)))
        def _():
            piece(o, m).wait_send()

        return carry

    def arrived(slot, carry):
        @pl.when(jnp.logical_not(jnp.logical_and(owner == d, slot == mine)))
        def _():
            remote(
                PS.at[0], PR.at[slot], pr_s.at[0], pr_r.at[slot], {"depth": d, "image": i}
            ).wait_recv()

        return carry

    lax.fori_loop(0, nd * ratio, arrived, 0)
    backward = row(i, 5 * bumps) > 0.5
    for part in range(ratio):
        for h in range(halves):
            rows = pl.ds(ROWS * h, ROWS)
            through = jnp.ones((ROWS, NZ), jnp.float32)
            colors = [jnp.zeros((ROWS, NZ), jnp.float32)] * 3
            for slab in range(nd):
                slot = slab * ratio + part
                local = [PR[slot, j, rows, :] for j in range(4)]
                through, colors = blend(backward, through, colors, local[3], local[:3])
            for j, value in enumerate(colors + [1.0 - through]):
                img[0, j, pl.ds(part * W + ROWS * h, ROWS), :] = value
    lax.fori_loop(0, ni, sent, 0)
    out.wait()


def on_device(populations, transfer, direction):
    nd, ni = lax.axis_size("depth"), lax.axis_size("image")
    count, X, W, NZ = populations.shape
    bumps = transfer.shape[2]
    assert transfer.shape[0] == 1 and ni % nd == 0 and W % ROWS == 0 and X % 8 == 0
    sizes = (nd, ni, X, W, NZ, bumps)
    ratio = ni // nd
    padded = W + 2 * ROWS
    f32 = jnp.float32
    table = -(-(5 * bumps + 1) // 8) * 8
    dma = pltpu.SemaphoreType.DMA
    return pl.pallas_call(
        functools.partial(kernel, sizes),
        out_shape=(
            jax.ShapeDtypeStruct(populations.shape, f32),
            jax.ShapeDtypeStruct((X, W, NZ), jnp.bfloat16),
            jax.ShapeDtypeStruct((1, 4, ratio * W, NZ), f32),
        ),
        in_specs=[
            pl.BlockSpec(memory_space=pl.ANY),
            pl.BlockSpec(memory_space=pltpu.SMEM),
            pl.BlockSpec(memory_space=pltpu.SMEM),
        ],
        out_specs=(
            pl.BlockSpec(memory_space=pl.ANY),
            pl.BlockSpec(memory_space=pltpu.VMEM),
            pl.BlockSpec(memory_space=pltpu.VMEM),
        ),
        scratch_shapes=[
            pltpu.VMEM((COUNT, X, W, NZ), f32),
            pltpu.VMEM((COUNT, X + 2, padded, NZ), f32),
            pltpu.VMEM((COUNT, X + 2, padded, NZ), f32),
            pltpu.VMEM((2, CROSS, X, NZ), f32),
            pltpu.VMEM((2, 2, CROSS, X, NZ), f32),
            pltpu.VMEM((4, 8, NZ), f32),
            pltpu.VMEM((2, 4, 8, NZ), f32),
            pltpu.VMEM((3, X + 2, padded, NZ), f32),
            pltpu.VMEM((2, 2, X, NZ), f32),
            pltpu.VMEM((2, 2, X, NZ), f32),
            pltpu.VMEM((X, W, NZ), f32),
            pltpu.VMEM((ni, table, NZ), f32),
            pltpu.VMEM((ni, 4, W, NZ), f32),
            pltpu.VMEM((nd * ratio, 4, W, NZ), f32),
            dma((4,)),
            dma(()),
            dma((STEPS, 8)),
            dma((STEPS, 8)),
            dma((4,)),
            dma((4,)),
            dma((ni,)),
            dma((ni,)),
            dma((ni,)),
            dma((nd * ratio,)),
        ],
        compiler_params=pltpu.CompilerParams(
            collective_id=0, has_side_effects=True, vmem_limit_bytes=56 << 20
        ),
    )(populations, transfer, direction)


def solution(mesh):
    in_specs = (P(None, "depth", "image", None), P("image", None, None), P("image"))
    out_specs = (
        P(None, "depth", "image", None),
        P("depth", "image", None),
        P("image", None, "depth", None),
    )
    return jax.shard_map(
        on_device, mesh=mesh, in_specs=in_specs, out_specs=out_specs, check_vma=False
    )
```

time: 379 us -> 79.3 us (0.21); the launches traced: 373 us -> 79.1 us
  other arithmetic: 154 us -> 0 us
  local copies, waits for them, and re-layouts: 101 us -> 7.75 us
  Pallas kernels: 0 us -> 70 us
  waiting for transfers between devices: 66.1 us -> 0 us
  starting transfers between devices: 34 us -> 0 us
  between operations: 17.6 us -> 1.3 us
    pallas_call x0 -> x1, Pallas kernels: none -> 70 us  [on_device(): pl.pallas_call(functools.partial(kernel, sizes), out_shape=(jax.ShapeDtyp...]
    concatenate x75 -> x0, local copies, waits for them, and re-layouts: 65.2 us -> none  [stream(): window = jnp.roll(window, shift_z, axis=2)]
    reduce_sum x3 -> x0, other arithmetic: 62.7 us -> none  [render_block(): jnp.sum(weight * emission[channel], axis=0)]
    ppermute x22 -> x0, waiting for transfers between devices: 38.8 us -> none  [the longest x10 23 us: with_halo(): before = lax.ppermute(last, axis, up)]
    ppermute x22 -> x0, starting transfers between devices: 33.9 us -> none  [the longest x10 28.8 us: with_halo(): after = lax.ppermute(first, axis, down)]
    unnamed x85 -> x0, other arithmetic: 30.9 us -> none
    all_gather x1 -> x0, waiting for transfers between devices: 27.3 us -> none  [on_device(): lax.all_gather(vorticity, 'image', axis=1, tiled=True)]
    slice x72 -> x0, local copies, waits for them, and re-layouts: 17 us -> none  [the longest x60 12.8 us: stream(): window = jnp.roll(window, shift_z, axis=2)]
  transfers between devices with their start and end apart: 23 -> 0, of which waited for: 16 -> 0; matrix products, arithmetic and copies ran while one was open for 14% -> 0% of each run, Pallas kernels for 0% -> 0%
where the time goes in v1:
time: 79.3 us; the launch traced here: 79.1 us
  Pallas kernels  70 us (88%)
  local copies, waits for them, and re-layouts  7.75 us (10%)
  between operations  1.3 us (2%)
    pallas_call x1, Pallas kernels, on_device(): pl.pallas_call(functools.partial(kernel, sizes), out_shape=(jax.ShapeDtyp...  70 us
    unnamed x8, local copies, waits for them, and re-layouts  7.75 us

profile of v1, /device:TPU:0, one launch (start us, length us, event | category | flops | bytes accessed | tf_op | source)
XLA Modules:
  0.0 79.1 jit_solution(7297845952190877941)
XLA Ops:
  1.3 1.3 %copy.6.par = f32[1,5,8]{2,1,0:T(8,128)} copy(f32[1,5,8]{2,0,1:T(1,128)} %param.4) | data formatting | bytes 320 | tf_op args[1]
  2.6 70.0 %shard_map.58 = (f32[19,32,16,128]{3,2,1,0:T(8,128)}, bf16[32,16,128]{2,1,0:T(8,128)(2,1)}, f32[1,4,32,128]{3,2,1,0:T(8,128)}) custom-call(f32[19,32,16,128]{3,2,1,0:T(8,128)} %f_hbm.1, f32[1,5,8]{2,1,0:T(8,128)} %copy.6.par, s32[1]{0:T(128)S(6)} %copy.10.direct), custom_call_target="tpu_custom_call" | custom-call | tf_op jit(solution)/shard_map/pallas_call | solution.py:484
  72.6 0.0 copy-start
  72.6 0.0 copy-start.1
  72.6 5.2 %copy.11 = f32[19,32,16,128]{3,2,1,0:T(8,128)} copy(f32[19,32,16,128]{3,2,1,0:T(8,128)} %get-tuple-element.6) | data formatting | bytes 9961472
  77.8 0.0 copy-done
  77.8 0.7 copy.12
  78.5 0.0 copy-done.1
  78.5 0.6 copy.13
Async XLA Ops:
  72.6 5.2 %copy-start = (bf16[32,16,128]{2,1,0:T(8,128)(2,1)S(1)}, bf16[32,16,128]{2,1,0:T(8,128)(2,1)}, u32[]{:S(2)}) copy-start(bf16[32,16,128]{2,1,0:T(8,128)(2,1)} %get-tuple-element.7) | copy-start | bytes 393220
  72.6 5.9 %copy-start.1 = (f32[1,4,32,128]{3,2,1,0:T(8,128)S(1)}, f32[1,4,32,128]{3,2,1,0:T(8,128)}, u32[]{:S(2)}) copy-start(f32[1,4,32,128]{3,2,1,0:T(8,128)} %get-tuple-element.8) | copy-start | bytes 196612

commit v2 on v1

--- a/solution.py
+++ b/solution.py
@@ -115,10 +115,9 @@
     f_hbm,
     par,
     direct,
-    fout,
+    F,
     vort,
     img,
-    F,
     A,
     B,
     SY,
@@ -129,11 +128,11 @@
     VS,
     VR,
     L,
+    PC,
     PA,
     PS,
     PR,
     in_sem,
-    out_sem,
     halo_s,
     halo_r,
     flow_s,
@@ -179,12 +178,13 @@
     lax.fori_loop(1, everyone, greet, 0)
 
     ray = X * nd
+    lane = lax.broadcasted_iota(jnp.int32, (8, NZ), 1)
+    entries = jnp.full((8, NZ), direct[0].astype(jnp.float32), jnp.float32)
     for k in range(bumps):
         for kind in range(5):
             factor = SCALE if kind == 0 else (LOG2E / ray if kind == 1 else 1.0)
-            value = par[0, kind, k] * factor
-            PA[i, pl.ds(kind * bumps + k, 1), :] = jnp.full((1, NZ), value, jnp.float32)
-    PA[i, pl.ds(5 * bumps, 1), :] = jnp.full((1, NZ), direct[0].astype(jnp.float32), jnp.float32)
+            entries = jnp.where(lane == kind * bumps + k, par[kind, 0, k] * factor, entries)
+    PC[i] = entries
 
     def to(cx, cy):
         return {"depth": lax.rem(d + cx + nd, nd), "image": lax.rem(i + cy + ni, ni)}
@@ -270,7 +270,7 @@
 
     pl.semaphore_wait(barrier, everyone - 1)
     shares = [
-        remote(PA.at[i], PA.at[i], pa_s.at[o], pa_r.at[o], to(0, o)) for o in range(1, ni)
+        remote(PC.at[i], PC.at[i], pa_s.at[o], pa_r.at[o], to(0, o)) for o in range(1, ni)
     ]
     exchange(A, 0)
     for copy in shares:
@@ -328,10 +328,18 @@
     ]
     for copy in flows:
         copy.start()
-    out = pltpu.make_async_copy(F, fout, out_sem)
-    out.start()
     for copy in shares:
         copy.wait()
+
+    def expand(m, carry):
+        for block in range(PA.shape[1] // 8):
+            line = lax.broadcasted_iota(jnp.int32, (8, NZ), 0) + 8 * block
+            chosen = jnp.where(lane == line, PC[m], 0.0)
+            value = jnp.sum(chosen, axis=1, keepdims=True)
+            PA[m, pl.ds(8 * block, 8), :] = jnp.broadcast_to(value, (8, NZ))
+        return carry
+
+    lax.fori_loop(0, ni, expand, 0)
     for copy in flows:
         copy.wait()
 
@@ -467,7 +475,6 @@
             for j, value in enumerate(colors + [1.0 - through]):
                 img[0, j, pl.ds(part * W + ROWS * h, ROWS), :] = value
     lax.fori_loop(0, ni, sent, 0)
-    out.wait()
 
 
 def on_device(populations, transfer, direction):
@@ -484,7 +491,7 @@
     return pl.pallas_call(
         functools.partial(kernel, sizes),
         out_shape=(
-            jax.ShapeDtypeStruct(populations.shape, f32),
+            pltpu.VMEM(populations.shape, f32),
             jax.ShapeDtypeStruct((X, W, NZ), jnp.bfloat16),
             jax.ShapeDtypeStruct((1, 4, ratio * W, NZ), f32),
         ),
@@ -494,12 +501,11 @@
             pl.BlockSpec(memory_space=pltpu.SMEM),
         ],
         out_specs=(
-            pl.BlockSpec(memory_space=pl.ANY),
+            pl.BlockSpec(memory_space=pltpu.VMEM),
             pl.BlockSpec(memory_space=pltpu.VMEM),
             pl.BlockSpec(memory_space=pltpu.VMEM),
         ),
         scratch_shapes=[
-            pltpu.VMEM((COUNT, X, W, NZ), f32),
             pltpu.VMEM((COUNT, X + 2, padded, NZ), f32),
             pltpu.VMEM((COUNT, X + 2, padded, NZ), f32),
             pltpu.VMEM((2, CROSS, X, NZ), f32),
@@ -510,11 +516,11 @@
             pltpu.VMEM((2, 2, X, NZ), f32),
             pltpu.VMEM((2, 2, X, NZ), f32),
             pltpu.VMEM((X, W, NZ), f32),
+            pltpu.VMEM((ni, 8, NZ), f32),
             pltpu.VMEM((ni, table, NZ), f32),
             pltpu.VMEM((ni, 4, W, NZ), f32),
             pltpu.VMEM((nd * ratio, 4, W, NZ), f32),
             dma((4,)),
-            dma(()),
             dma((STEPS, 8)),
             dma((STEPS, 8)),
             dma((4,)),
@@ -527,7 +533,7 @@
         compiler_params=pltpu.CompilerParams(
             collective_id=0, has_side_effects=True, vmem_limit_bytes=56 << 20
         ),
-    )(populations, transfer, direction)
+    )(populations, transfer.transpose(1, 0, 2), direction)
 
 
 def solution(mesh):

time: 79.3 us -> 75 us (0.946)
  local copies, waits for them, and re-layouts: 7.75 us -> 3.57 us
    unnamed x8 -> x7, local copies, waits for them, and re-layouts: 7.75 us -> 3.57 us
where the time goes in v2:
time: 75 us; the launch traced here: 74.8 us
  Pallas kernels  69.9 us (93%)
  local copies, waits for them, and re-layouts  3.57 us (5%)
  between operations  1.3 us (2%)
    pallas_call x1, Pallas kernels, on_device(): pl.pallas_call(functools.partial(kernel, sizes), out_shape=(pltpu.VMEM(po...  69.9 us
    unnamed x7, local copies, waits for them, and re-layouts  3.57 us

profile of v2, /device:TPU:0, one launch (start us, length us, event | category | flops | bytes accessed | tf_op | source)
XLA Modules:
  0.0 74.8 jit_solution(15515964057526376811)
XLA Ops:
  1.3 69.9 %shard_map.58 = (f32[19,32,16,128]{3,2,1,0:T(8,128)S(1)}, bf16[32,16,128]{2,1,0:T(8,128)(2,1)}, f32[1,4,32,128]{3,2,1,0:T(8,128)}) custom-call(f32[19,32,16,128]{3,2,1,0:T(8,128)} %f_hbm.1, f32[5,1,8]{2,1,0:T(1,128)} %bitcast.1, s32[1]{0:T(128)S(6)} %copy.10.direct), custom_call_target="tpu_custom_call" | custom-call | tf_op jit(solution)/shard_map/pallas_call | solution.py:491
  71.2 0.0 copy-start
  71.2 0.0 copy-start.1
  71.2 2.3 %copy.9 = f32[19,32,16,128]{3,2,1,0:T(8,128)} copy(f32[19,32,16,128]{3,2,1,0:T(8,128)S(1)} %get-tuple-element.3) | data formatting | bytes 9961472
  73.5 0.0 copy-done
  73.5 0.7 copy.11
  74.1 0.0 copy-done.1
  74.1 0.6 copy.12
Async XLA Ops:
  71.2 2.3 %copy-start = (bf16[32,16,128]{2,1,0:T(8,128)(2,1)S(1)}, bf16[32,16,128]{2,1,0:T(8,128)(2,1)}, u32[]{:S(2)}) copy-start(bf16[32,16,128]{2,1,0:T(8,128)(2,1)} %get-tuple-element.10) | copy-start | bytes 393220
  71.2 2.9 %copy-start.1 = (f32[1,4,32,128]{3,2,1,0:T(8,128)S(1)}, f32[1,4,32,128]{3,2,1,0:T(8,128)}, u32[]{:S(2)}) copy-start(f32[1,4,32,128]{3,2,1,0:T(8,128)} %get-tuple-element.11) | copy-start | bytes 196612

commit v3 on v2

--- a/solution.py
+++ b/solution.py
@@ -120,6 +120,7 @@
     img,
     A,
     B,
+    E,
     SY,
     RY,
     SC,
@@ -199,42 +200,86 @@
             device_id_type=MESH,
         )
 
-    def store(D, x, h, values):
-        for number in range(COUNT):
-            D[SLOT[number], x + 1, pl.ds(LOW + ROWS * h, ROWS), :] = values[number]
-        if h == 0:
-            for j, number in enumerate(DOWN_Y):
-                SY[0, j, pl.ds(x, 1), :] = values[number][0:1]
-        if h == halves - 1:
-            for j, number in enumerate(UP_Y):
-                SY[1, j, pl.ds(x, 1), :] = values[number][ROWS - 1 : ROWS]
-
-    def streamed(S, x, h):
+    starts = list(range(1, W - 1 - ROWS, ROWS)) + [W - 1 - ROWS]
+    edge_rows = (0, W - 1)
+    outward = (DOWN_Y, UP_Y)
+    inward = (UP_Y, DOWN_Y)
+
+    def pack(b, x, start, values):
+        if start == 1:
+            for number in DOWN_Y:
+                E[b, 0, SLOT[number], pl.ds(ROWS + x, 1), :] = values[number][0:1]
+        if start == W - 1 - ROWS:
+            for number in UP_Y:
+                E[b, 1, SLOT[number], pl.ds(ROWS + x, 1), :] = values[number][ROWS - 1 : ROWS]
+
+    def streamed(S, x, start):
         field = []
         for number in range(COUNT):
             cx, cy, cz = lattice_velocities[number]
-            value = S[SLOT[number], x + 1 - cx, pl.ds(LOW + ROWS * h - cy, ROWS), :]
+            value = S[SLOT[number], x + 1 - cx, pl.ds(LOW + start - cy, ROWS), :]
             if cz:
                 value = pltpu.roll(value, cz % NZ, 1)
             field.append(value)
         return field
 
+    def edge_streamed(b, side, x):
+        field = []
+        for number in range(COUNT):
+            cx, _, cz = lattice_velocities[number]
+            rows = slice(ROWS + x - cx, 2 * ROWS + x - cx)
+            if number in inward[side]:
+                value = RY[b, side, inward[side].index(number), rows, :]
+            else:
+                value = E[b, side, SLOT[number], rows, :]
+            if cz:
+                value = pltpu.roll(value, cz % NZ, 1)
+            field.append(value)
+        return field
+
+    def update(S, D, b, x):
+        for start in starts:
+            values = collide(streamed(S, x, start))
+            for number in range(COUNT):
+                D[SLOT[number], x + 1, pl.ds(LOW + start, ROWS), :] = values[number]
+            pack(b, x, start, values)
+
+    def put_edges(D, b, side, x, values):
+        row = LOW + edge_rows[side]
+        for number in range(COUNT):
+            cx, cy, _ = lattice_velocities[number]
+            value = values[number]
+            if number in inward[side]:
+                for r in range(ROWS):
+                    D[SLOT[number], x + r + 1, row : row + 1, :] = value[r : r + 1]
+                continue
+            if cy == 0:
+                E[b, side, SLOT[number], ROWS + x : 2 * ROWS + x, :] = value
+            else:
+                SY[side, outward[side].index(number), x : x + ROWS, :] = value
+            if cx == 1 and x == X - ROWS:
+                D[SLOT[number], X, row : row + 1, :] = value[ROWS - 1 : ROWS]
+            if cx == -1 and x == 0:
+                D[SLOT[number], 1, row : row + 1, :] = value[0:1]
+
+    inner = pl.ds(LOW, W)
+
     def exchange(D, turn):
         slot = turn % 2
         for k, number in enumerate(CORNERS):
             cx, cy, _ = lattice_velocities[number]
-            group = UP_Y if cy == 1 else DOWN_Y
+            side = 1 if cy == 1 else 0
             edge = X - 1 if cx == 1 else 0
-            SC[k, 0:1, :] = SY[1 if cy == 1 else 0, group.index(number), edge : edge + 1, :]
-        inner = pl.ds(LOW, W)
+            SC[k, 0:1, :] = SY[side, outward[side].index(number), edge : edge + 1, :]
         copies = []
 
         def add(src, dst, target):
             k = len(copies)
             copies.append(remote(src, dst, halo_s.at[turn, k], halo_r.at[turn, k], target))
 
-        add(SY.at[1], RY.at[slot, 1], to(0, 1))
-        add(SY.at[0], RY.at[slot, 0], to(0, -1))
+        body = pl.ds(ROWS, X)
+        add(SY.at[1], RY.at[slot, 0, :, body], to(0, 1))
+        add(SY.at[0], RY.at[slot, 1, :, body], to(0, -1))
         for k, number in enumerate(CORNERS):
             cx, cy, _ = lattice_velocities[number]
             add(SC.at[k], RC.at[slot, k], to(cx, cy))
@@ -242,26 +287,48 @@
         add(D.at[pl.ds(CROSS, CROSS), 1, inner], D.at[pl.ds(CROSS, CROSS), X + 1, inner], to(-1, 0))
         for copy in copies:
             copy.start()
+        return copies
+
+    def finish(copies, D, turn):
+        slot = turn % 2
         for copy in copies:
             copy.wait()
-
-        def unpack(x, carry):
-            for j, number in enumerate(UP_Y):
-                D[SLOT[number], x + 1, pl.ds(LOW - 1, 1), :] = RY[slot, 1, j, pl.ds(x, 1), :]
-            for j, number in enumerate(DOWN_Y):
-                D[SLOT[number], x + 1, pl.ds(LOW + W, 1), :] = RY[slot, 0, j, pl.ds(x, 1), :]
-            return carry
-
-        lax.fori_loop(0, X, unpack, 0)
-        for k, number in enumerate(CORNERS):
+        for number in range(COUNT):
             cx, cy, _ = lattice_velocities[number]
-            row = LOW - 1 if cy == 1 else LOW + W
-            D[SLOT[number], 0 if cx == 1 else X + 1, row : row + 1, :] = RC[slot, k, 0:1, :]
+            if cx == 0:
+                continue
+            plane, place = (0, ROWS - 1) if cx == 1 else (X + 1, ROWS + X)
+            for side in range(2):
+                if number in inward[side]:
+                    k = CORNERS.index(number)
+                    j = inward[side].index(number)
+                    RY[slot, side, j, place : place + 1, :] = RC[slot, k, 0:1, :]
+                else:
+                    row = LOW + edge_rows[side] - cy
+                    E[slot, side, SLOT[number], place : place + 1, :] = D[
+                        SLOT[number], plane, row : row + 1, :
+                    ]
 
     def first(x, carry):
         for h in range(halves):
             field = [F[number, x, pl.ds(ROWS * h, ROWS), :] for number in range(COUNT)]
-            store(A, x, h, collide(field))
+            values = collide(field)
+            for number in range(COUNT):
+                A[SLOT[number], x + 1, pl.ds(LOW + ROWS * h, ROWS), :] = values[number]
+            for side, edge in ((0, 0), (1, ROWS - 1)):
+                if h != (0 if side == 0 else halves - 1):
+                    continue
+                near = 1 if side == 0 else ROWS - 2
+                for number in range(COUNT):
+                    if lattice_velocities[number][1] == 0:
+                        E[0, side, SLOT[number], pl.ds(ROWS + x, 1), :] = values[number][
+                            edge : edge + 1
+                        ]
+                for j, number in enumerate(outward[side]):
+                    SY[side, j, pl.ds(x, 1), :] = values[number][edge : edge + 1]
+                    E[0, side, SLOT[number], pl.ds(ROWS + x, 1), :] = values[number][
+                        near : near + 1
+                    ]
         return carry
 
     for c in range(chunks):
@@ -272,42 +339,58 @@
     shares = [
         remote(PC.at[i], PC.at[i], pa_s.at[o], pa_r.at[o], to(0, o)) for o in range(1, ni)
     ]
-    exchange(A, 0)
+    copies = exchange(A, 0)
     for copy in shares:
         copy.start()
 
     source, target = A, B
     for turn in range(1, STEPS):
 
-        def middle(x, carry, source=source, target=target):
-            for h in range(halves):
-                store(target, x, h, collide(streamed(source, x, h)))
+        def middle(x, carry, source=source, target=target, turn=turn):
+            update(source, target, turn % 2, x)
             return carry
 
-        lax.fori_loop(0, X, middle, 0)
-        exchange(target, turn)
+        lax.fori_loop(1, X - 1, middle, 0)
+        finish(copies, source, turn - 1)
+        for x in (0, X - 1):
+            middle(x, 0)
+        for side in range(2):
+            for x in range(0, X, ROWS):
+                put_edges(target, turn % 2, side, x, collide(edge_streamed((turn - 1) % 2, side, x)))
+        copies = exchange(target, turn)
         source, target = target, source
 
+    def flow_of(field):
+        density, momentum = moments(field)
+        inverse = 1.0 / density
+        return [momentum[axis] * inverse for axis in (1, 2, 0)]
+
     def last(x, carry):
-        for h in range(halves):
-            field = streamed(source, x, h)
+        for start in starts:
+            field = streamed(source, x, start)
             for number in range(COUNT):
-                F[number, x, pl.ds(ROWS * h, ROWS), :] = field[number]
-            density, momentum = moments(field)
-            inverse = 1.0 / density
-            flow = [part * inverse for part in momentum]
-            for place, axis in enumerate((1, 2, 0)):
-                U[place, x + 1, pl.ds(LOW + ROWS * h, ROWS), :] = flow[axis]
-            if h == 0:
-                VS[0, 0, pl.ds(x, 1), :] = flow[2][0:1]
-                VS[0, 1, pl.ds(x, 1), :] = flow[0][0:1]
-            if h == halves - 1:
-                VS[1, 0, pl.ds(x, 1), :] = flow[2][ROWS - 1 : ROWS]
-                VS[1, 1, pl.ds(x, 1), :] = flow[0][ROWS - 1 : ROWS]
-        return carry
-
-    lax.fori_loop(0, X, last, 0)
-    inner = pl.ds(LOW, W)
+                F[number, x, pl.ds(start, ROWS), :] = field[number]
+            for place, value in enumerate(flow_of(field)):
+                U[place, x + 1, pl.ds(LOW + start, ROWS), :] = value
+        return carry
+
+    lax.fori_loop(1, X - 1, last, 0)
+    finish(copies, source, STEPS - 1)
+    for x in (0, X - 1):
+        last(x, 0)
+    for side in range(2):
+        row = edge_rows[side]
+        for x in range(0, X, ROWS):
+            field = edge_streamed((STEPS - 1) % 2, side, x)
+            for number in range(COUNT):
+                for r in range(ROWS):
+                    F[number, x + r, row : row + 1, :] = field[number][r : r + 1]
+            flow = flow_of(field)
+            for place, value in enumerate(flow):
+                for r in range(ROWS):
+                    U[place, x + r + 1, LOW + row : LOW + row + 1, :] = value[r : r + 1]
+            VS[side, 0, x : x + ROWS, :] = flow[1]
+            VS[side, 1, x : x + ROWS, :] = flow[2]
     flows = [
         remote(VS.at[1], VR.at[1], flow_s.at[0], flow_r.at[0], to(0, 1)),
         remote(VS.at[0], VR.at[0], flow_s.at[1], flow_r.at[1], to(0, -1)),
@@ -481,7 +564,7 @@
     nd, ni = lax.axis_size("depth"), lax.axis_size("image")
     count, X, W, NZ = populations.shape
     bumps = transfer.shape[2]
-    assert transfer.shape[0] == 1 and ni % nd == 0 and W % ROWS == 0 and X % 8 == 0
+    assert transfer.shape[0] == 1 and ni % nd == 0 and W % ROWS == 0 and W >= 2 * ROWS and X % 8 == 0
     sizes = (nd, ni, X, W, NZ, bumps)
     ratio = ni // nd
     padded = W + 2 * ROWS
@@ -508,8 +591,9 @@
         scratch_shapes=[
             pltpu.VMEM((COUNT, X + 2, padded, NZ), f32),
             pltpu.VMEM((COUNT, X + 2, padded, NZ), f32),
+            pltpu.VMEM((2, 2, COUNT, X + 2 * ROWS, NZ), f32),
             pltpu.VMEM((2, CROSS, X, NZ), f32),
-            pltpu.VMEM((2, 2, CROSS, X, NZ), f32),
+            pltpu.VMEM((2, 2, CROSS, X + 2 * ROWS, NZ), f32),
             pltpu.VMEM((4, 8, NZ), f32),
             pltpu.VMEM((2, 4, 8, NZ), f32),
             pltpu.VMEM((3, X + 2, padded, NZ), f32),

time: 75 us -> 60.9 us (0.81)
  Pallas kernels: 69.9 us -> 55.9 us
    pallas_call x1, Pallas kernels: 69.9 us -> 55.9 us  [on_device(): pl.pallas_call(functools.partial(kernel, sizes), out_shape=(pltpu.VMEM(po...]
where the time goes in v3:
time: 60.9 us; the launch traced here: 60.8 us
  Pallas kernels  55.9 us (92%)
  local copies, waits for them, and re-layouts  3.57 us (6%)
  between operations  1.3 us (2%)
    pallas_call x1, Pallas kernels, on_device(): pl.pallas_call(functools.partial(kernel, sizes), out_shape=(pltpu.VMEM(po...  55.9 us
    unnamed x7, local copies, waits for them, and re-layouts  3.57 us

profile of v3, /device:TPU:0, one launch (start us, length us, event | category | flops | bytes accessed | tf_op | source)
XLA Modules:
  0.0 60.8 jit_solution(13770135764644831936)
XLA Ops:
  1.3 55.9 %shard_map.58 = (f32[19,32,16,128]{3,2,1,0:T(8,128)S(1)}, bf16[32,16,128]{2,1,0:T(8,128)(2,1)}, f32[1,4,32,128]{3,2,1,0:T(8,128)}) custom-call(f32[19,32,16,128]{3,2,1,0:T(8,128)} %f_hbm.1, f32[5,1,8]{2,1,0:T(1,128)} %bitcast.1, s32[1]{0:T(128)S(6)} %copy.10.direct), custom_call_target="tpu_custom_call" | custom-call | tf_op jit(solution)/shard_map/pallas_call | solution.py:574
  57.2 0.0 copy-start
  57.2 0.0 copy-start.1
  57.2 2.3 %copy.9 = f32[19,32,16,128]{3,2,1,0:T(8,128)} copy(f32[19,32,16,128]{3,2,1,0:T(8,128)S(1)} %get-tuple-element.3) | data formatting | bytes 9961472
  59.5 0.0 copy-done
  59.5 0.7 %copy.11 = bf16[32,16,128]{2,1,0:T(8,128)(2,1)} copy(bf16[32,16,128]{2,1,0:T(8,128)(2,1)S(1)} %copy-done) | data formatting | bytes 262144
  60.1 0.0 copy-done.1
  60.1 0.6 %copy.12 = f32[1,4,32,128]{3,2,1,0:T(8,128)} copy(f32[1,4,32,128]{3,2,1,0:T(8,128)S(1)} %copy-done.1) | data formatting | bytes 131072
Async XLA Ops:
  57.2 2.3 %copy-start = (bf16[32,16,128]{2,1,0:T(8,128)(2,1)S(1)}, bf16[32,16,128]{2,1,0:T(8,128)(2,1)}, u32[]{:S(2)}) copy-start(bf16[32,16,128]{2,1,0:T(8,128)(2,1)} %get-tuple-element.10) | copy-start | bytes 393220
  57.2 2.9 %copy-start.1 = (f32[1,4,32,128]{3,2,1,0:T(8,128)S(1)}, f32[1,4,32,128]{3,2,1,0:T(8,128)}, u32[]{:S(2)}) copy-start(f32[1,4,32,128]{3,2,1,0:T(8,128)} %get-tuple-element.11) | copy-start | bytes 196612

commit v4 on v3

--- a/solution.py
+++ b/solution.py
@@ -129,6 +129,7 @@
     VS,
     VR,
     L,
+    G,
     PC,
     PA,
     PS,
@@ -185,7 +186,16 @@
         for kind in range(5):
             factor = SCALE if kind == 0 else (LOG2E / ray if kind == 1 else 1.0)
             entries = jnp.where(lane == kind * bumps + k, par[kind, 0, k] * factor, entries)
-    PC[i] = entries
+    gain = pltpu.roll(entries, bumps, 1)
+    shift = gain * gain - jnp.log2(entries)
+    ratios = entries / gain
+    for kind in (3, 4):
+        ratios = jnp.where(
+            lane < kind * bumps, ratios, entries / pltpu.roll(entries, (kind - 1) * bumps, 1)
+        )
+    table = jnp.where(lane < 2 * bumps, shift, ratios)
+    table = jnp.where(lane < bumps, 2.0 * entries, table)
+    PC[i] = jnp.where(lane < 5 * bumps, table, entries)[0:1]
 
     def to(cx, cy):
         return {"depth": lax.rem(d + cx + nd, nd), "image": lax.rem(i + cy + ni, ni)}
@@ -264,18 +274,19 @@
 
     inner = pl.ds(LOW, W)
 
-    def exchange(D, turn):
+    def exchange(D, turn, columns=None):
         slot = turn % 2
         for k, number in enumerate(CORNERS):
             cx, cy, _ = lattice_velocities[number]
             side = 1 if cy == 1 else 0
             edge = X - 1 if cx == 1 else 0
-            SC[k, 0:1, :] = SY[side, outward[side].index(number), edge : edge + 1, :]
+            SC[k] = SY[side, outward[side].index(number), edge : edge + 1, :]
         copies = []
 
         def add(src, dst, target):
             k = len(copies)
             copies.append(remote(src, dst, halo_s.at[turn, k], halo_r.at[turn, k], target))
+            copies[-1].start()
 
         body = pl.ds(ROWS, X)
         add(SY.at[1], RY.at[slot, 0, :, body], to(0, 1))
@@ -283,10 +294,11 @@
         for k, number in enumerate(CORNERS):
             cx, cy, _ = lattice_velocities[number]
             add(SC.at[k], RC.at[slot, k], to(cx, cy))
+        if columns is not None:
+            for x in (0, X - 1):
+                columns(x, 0)
         add(D.at[pl.ds(0, CROSS), X, inner], D.at[pl.ds(0, CROSS), 0, inner], to(1, 0))
         add(D.at[pl.ds(CROSS, CROSS), 1, inner], D.at[pl.ds(CROSS, CROSS), X + 1, inner], to(-1, 0))
-        for copy in copies:
-            copy.start()
         return copies
 
     def finish(copies, D, turn):
@@ -302,7 +314,7 @@
                 if number in inward[side]:
                     k = CORNERS.index(number)
                     j = inward[side].index(number)
-                    RY[slot, side, j, place : place + 1, :] = RC[slot, k, 0:1, :]
+                    RY[slot, side, j, place : place + 1, :] = RC[slot, k]
                 else:
                     row = LOW + edge_rows[side] - cy
                     E[slot, side, SLOT[number], place : place + 1, :] = D[
@@ -352,12 +364,10 @@
 
         lax.fori_loop(1, X - 1, middle, 0)
         finish(copies, source, turn - 1)
-        for x in (0, X - 1):
-            middle(x, 0)
         for side in range(2):
             for x in range(0, X, ROWS):
                 put_edges(target, turn % 2, side, x, collide(edge_streamed((turn - 1) % 2, side, x)))
-        copies = exchange(target, turn)
+        copies = exchange(target, turn, middle)
         source, target = target, source
 
     def flow_of(field):
@@ -382,9 +392,6 @@
         row = edge_rows[side]
         for x in range(0, X, ROWS):
             field = edge_streamed((STEPS - 1) % 2, side, x)
-            for number in range(COUNT):
-                for r in range(ROWS):
-                    F[number, x + r, row : row + 1, :] = field[number][r : r + 1]
             flow = flow_of(field)
             for place, value in enumerate(flow):
                 for r in range(ROWS):
@@ -411,13 +418,20 @@
     ]
     for copy in flows:
         copy.start()
+    for side in range(2):
+        row = edge_rows[side]
+        for x in range(0, X, ROWS):
+            field = edge_streamed((STEPS - 1) % 2, side, x)
+            for number in range(COUNT):
+                for r in range(ROWS):
+                    F[number, x + r, row : row + 1, :] = field[number][r : r + 1]
     for copy in shares:
         copy.wait()
 
     def expand(m, carry):
         for block in range(PA.shape[1] // 8):
             line = lax.broadcasted_iota(jnp.int32, (8, NZ), 0) + 8 * block
-            chosen = jnp.where(lane == line, PC[m], 0.0)
+            chosen = jnp.where(lane == line, jnp.broadcast_to(PC[m], (8, NZ)), 0.0)
             value = jnp.sum(chosen, axis=1, keepdims=True)
             PA[m, pl.ds(8 * block, 8), :] = jnp.broadcast_to(value, (8, NZ))
         return carry
@@ -453,7 +467,9 @@
         rounded = size.astype(jnp.bfloat16)
         vort[x] = rounded
         value = rounded.astype(jnp.float32)
-        L[x] = (value / (value + level_offset)) * SCALE
+        level = (value / (value + level_offset)) * SCALE
+        L[x] = level
+        G[x] = jnp.exp2(-(level * level))
         return carry
 
     lax.fori_loop(0, X, spin, 0)
@@ -489,17 +505,19 @@
             totals = [[None] * 4 for h in range(halves)]
             for k in range(bumps):
                 centre = row(m, k)
-                gains = [row(m, (1 + j) * bumps + k) for j in range(4)]
+                shift = row(m, bumps + k)
+                gains = [row(m, (1 + j) * bumps + k) for j in range(1, 4)]
                 for h in range(halves):
-                    offset = levels[h] - centre
-                    bump = jnp.exp2(-(offset * offset))
+                    bump = jnp.exp2(levels[h] * centre - shift)
                     for j in range(4):
-                        term = gains[j] * bump
+                        term = gains[j - 1] * bump if j else bump
                         totals[h][j] = term if k == 0 else totals[h][j] + term
             for h in range(halves):
                 through, colors = state[4 * h], state[4 * h + 1 : 4 * h + 4]
-                local = jnp.exp2(-totals[h][0])
-                alpha = 1.0 - local
+                common = G[x, pl.ds(ROWS * h, ROWS), :]
+                optical = totals[h][0] * common
+                local = jnp.exp2(-optical)
+                alpha = (1.0 - local) * common
                 shades = [alpha * total for total in totals[h][1:]]
                 through, colors = blend(backward, through, colors, local, shades)
                 new += [through] + list(colors)
@@ -594,13 +612,14 @@
             pltpu.VMEM((2, 2, COUNT, X + 2 * ROWS, NZ), f32),
             pltpu.VMEM((2, CROSS, X, NZ), f32),
             pltpu.VMEM((2, 2, CROSS, X + 2 * ROWS, NZ), f32),
-            pltpu.VMEM((4, 8, NZ), f32),
-            pltpu.VMEM((2, 4, 8, NZ), f32),
+            pltpu.VMEM((4, 1, NZ), f32),
+            pltpu.VMEM((2, 4, 1, NZ), f32),
             pltpu.VMEM((3, X + 2, padded, NZ), f32),
             pltpu.VMEM((2, 2, X, NZ), f32),
             pltpu.VMEM((2, 2, X, NZ), f32),
             pltpu.VMEM((X, W, NZ), f32),
-            pltpu.VMEM((ni, 8, NZ), f32),
+            pltpu.VMEM((X, W, NZ), f32),
+            pltpu.VMEM((ni, 1, NZ), f32),
             pltpu.VMEM((ni, table, NZ), f32),
             pltpu.VMEM((ni, 4, W, NZ), f32),
             pltpu.VMEM((nd * ratio, 4, W, NZ), f32),

time: 60.9 us -> 57.9 us (0.951)
  Pallas kernels: 55.9 us -> 52.9 us
    pallas_call x1, Pallas kernels: 55.9 us -> 52.9 us  [on_device(): pl.pallas_call(functools.partial(kernel, sizes), out_shape=(pltpu.VMEM(po...]
where the time goes in v4:
time: 57.9 us; the launch traced here: 57.8 us
  Pallas kernels  52.9 us (91%)
  local copies, waits for them, and re-layouts  3.57 us (6%)
  between operations  1.3 us (2%)
    pallas_call x1, Pallas kernels, on_device(): pl.pallas_call(functools.partial(kernel, sizes), out_shape=(pltpu.VMEM(po...  52.9 us
    unnamed x7, local copies, waits for them, and re-layouts  3.57 us

profile of v4, /device:TPU:0, one launch (start us, length us, event | category | flops | bytes accessed | tf_op | source)
XLA Modules:
  0.0 57.8 jit_solution(845069912177773157)
XLA Ops:
  1.3 52.9 %shard_map.58 = (f32[19,32,16,128]{3,2,1,0:T(8,128)S(1)}, bf16[32,16,128]{2,1,0:T(8,128)(2,1)}, f32[1,4,32,128]{3,2,1,0:T(8,128)}) custom-call(f32[19,32,16,128]{3,2,1,0:T(8,128)} %f_hbm.1, f32[5,1,8]{2,1,0:T(1,128)} %bitcast.1, s32[1]{0:T(128)S(6)} %copy.10.direct), custom_call_target="tpu_custom_call" | custom-call | tf_op jit(solution)/shard_map/pallas_call | solution.py:592
  54.2 0.0 copy-start
  54.2 0.0 copy-start.1
  54.2 2.3 %copy.9 = f32[19,32,16,128]{3,2,1,0:T(8,128)} copy(f32[19,32,16,128]{3,2,1,0:T(8,128)S(1)} %get-tuple-element.3) | data formatting | bytes 9961472
  56.5 0.0 copy-done
  56.5 0.7 %copy.11 = bf16[32,16,128]{2,1,0:T(8,128)(2,1)} copy(bf16[32,16,128]{2,1,0:T(8,128)(2,1)S(1)} %copy-done) | data formatting | bytes 262144
  57.1 0.0 copy-done.1
  57.1 0.6 %copy.12 = f32[1,4,32,128]{3,2,1,0:T(8,128)} copy(f32[1,4,32,128]{3,2,1,0:T(8,128)S(1)} %copy-done.1) | data formatting | bytes 131072
Async XLA Ops:
  54.2 2.3 %copy-start = (bf16[32,16,128]{2,1,0:T(8,128)(2,1)S(1)}, bf16[32,16,128]{2,1,0:T(8,128)(2,1)}, u32[]{:S(2)}) copy-start(bf16[32,16,128]{2,1,0:T(8,128)(2,1)} %get-tuple-element.10) | copy-start | bytes 393220
  54.2 2.9 %copy-start.1 = (f32[1,4,32,128]{3,2,1,0:T(8,128)S(1)}, f32[1,4,32,128]{3,2,1,0:T(8,128)}, u32[]{:S(2)}) copy-start(f32[1,4,32,128]{3,2,1,0:T(8,128)} %get-tuple-element.11) | copy-start | bytes 196612

commit v5 on v4

--- a/solution.py
+++ b/solution.py
@@ -436,7 +436,7 @@
             PA[m, pl.ds(8 * block, 8), :] = jnp.broadcast_to(value, (8, NZ))
         return carry
 
-    lax.fori_loop(0, ni, expand, 0)
+    lax.fori_loop(0, ni, expand, 0, unroll=2)
     for copy in flows:
         copy.wait()
 
@@ -472,7 +472,7 @@
         G[x] = jnp.exp2(-(level * level))
         return carry
 
-    lax.fori_loop(0, X, spin, 0)
+    lax.fori_loop(0, X, spin, 0, unroll=2)
 
     owner = i // ratio
     mine = d * ratio + lax.rem(i, ratio)
@@ -525,7 +525,7 @@
 
         zero = jnp.zeros((ROWS, NZ), jnp.float32)
         start = (jnp.ones((ROWS, NZ), jnp.float32), zero, zero, zero) * halves
-        state = lax.fori_loop(0, X, along, start)
+        state = lax.fori_loop(0, X, along, start, unroll=2)
         for h in range(halves):
             through, colors = state[4 * h], state[4 * h + 1 : 4 * h + 4]
             for j, value in enumerate(list(colors) + [through]):

time: 57.9 us -> 55.2 us (0.953)
  Pallas kernels: 52.9 us -> 50.2 us
    pallas_call x1, Pallas kernels: 52.9 us -> 50.2 us  [on_device(): pl.pallas_call(functools.partial(kernel, sizes), out_shape=(pltpu.VMEM(po...]
where the time goes in v5:
time: 55.2 us; the launch traced here: 55 us
  Pallas kernels  50.2 us (91%)
  local copies, waits for them, and re-layouts  3.57 us (6%)
  between operations  1.3 us (2%)
    pallas_call x1, Pallas kernels, on_device(): pl.pallas_call(functools.partial(kernel, sizes), out_shape=(pltpu.VMEM(po...  50.2 us
    unnamed x7, local copies, waits for them, and re-layouts  3.57 us

profile of v5, /device:TPU:0, one launch (start us, length us, event | category | flops | bytes accessed | tf_op | source)
XLA Modules:
  0.0 55.0 jit_solution(16458200533668422152)
XLA Ops:
  1.3 50.2 %shard_map.58 = (f32[19,32,16,128]{3,2,1,0:T(8,128)S(1)}, bf16[32,16,128]{2,1,0:T(8,128)(2,1)}, f32[1,4,32,128]{3,2,1,0:T(8,128)}) custom-call(f32[19,32,16,128]{3,2,1,0:T(8,128)} %f_hbm.1, f32[5,1,8]{2,1,0:T(1,128)} %bitcast.1, s32[1]{0:T(128)S(6)} %copy.10.direct), custom_call_target="tpu_custom_call" | custom-call | tf_op jit(solution)/shard_map/pallas_call | solution.py:592
  51.5 0.0 copy-start
  51.5 0.0 copy-start.1
  51.5 2.3 %copy.9 = f32[19,32,16,128]{3,2,1,0:T(8,128)} copy(f32[19,32,16,128]{3,2,1,0:T(8,128)S(1)} %get-tuple-element.3) | data formatting | bytes 9961472
  53.7 0.0 copy-done
  53.7 0.7 %copy.11 = bf16[32,16,128]{2,1,0:T(8,128)(2,1)} copy(bf16[32,16,128]{2,1,0:T(8,128)(2,1)S(1)} %copy-done) | data formatting | bytes 262144
  54.4 0.0 copy-done.1
  54.4 0.6 %copy.12 = f32[1,4,32,128]{3,2,1,0:T(8,128)} copy(f32[1,4,32,128]{3,2,1,0:T(8,128)S(1)} %copy-done.1) | data formatting | bytes 131072
Async XLA Ops:
  51.5 2.3 %copy-start = (bf16[32,16,128]{2,1,0:T(8,128)(2,1)S(1)}, bf16[32,16,128]{2,1,0:T(8,128)(2,1)}, u32[]{:S(2)}) copy-start(bf16[32,16,128]{2,1,0:T(8,128)(2,1)} %get-tuple-element.10) | copy-start | bytes 393220
  51.5 2.9 %copy-start.1 = (f32[1,4,32,128]{3,2,1,0:T(8,128)S(1)}, f32[1,4,32,128]{3,2,1,0:T(8,128)}, u32[]{:S(2)}) copy-start(f32[1,4,32,128]{3,2,1,0:T(8,128)} %get-tuple-element.11) | copy-start | bytes 196612
